TPU v7x, 256 devices: a whole 4x4x8 slice. The times are simulated.
256 devices in a mesh: section: 2 (over core), tp: 8 (over z), mem: 16 (over y, x).
Axes of the slice: x: 4, y: 4, z: 8, core: 2. Of those that a mesh axis runs over, the one named last changes fastest.
Arguments:
- hidden_in: bfloat16 [32, 8192], P(None, 'mem'), may hold values from -12 to 12
- lengths: int32 [32], replicated, may hold values from 1 to 4096, as said below
- owner_order: int32 [32], replicated, may hold values from 0 to 31, each once
- attn_gain: bfloat16 [2, 8192], P('section', 'mem'), may hold values from 0.25 to 1.75
- w_query: bfloat16 [2, 8192, 8192], P('section', 'mem', 'tp'), may hold values from -0.0625 to 0.0625
- w_key: bfloat16 [2, 8192, 1024], P('section', 'mem', 'tp'), may hold values from -0.0625 to 0.0625
- w_value: bfloat16 [2, 8192, 1024], P('section', 'mem', 'tp'), may hold values from -0.0625 to 0.0625
- w_out: bfloat16 [2, 8192, 8192], P('section', 'tp', 'mem'), may hold values from -0.0625 to 0.0625
- ffn_gain: bfloat16 [2, 8192], P('section', 'mem'), may hold values from 0.25 to 1.75
- w_gate: bfloat16 [2, 8192, 14336], P('section', 'mem', 'tp'), may hold values from -0.0625 to 0.0625
- w_up: bfloat16 [2, 8192, 14336], P('section', 'mem', 'tp'), may hold values from -0.0625 to 0.0625
- w_down: bfloat16 [2, 14336, 8192], P('section', 'tp', 'mem'), may hold values from -0.046875 to 0.046875
- key_cache: bfloat16 [2, 32, 4096, 1024], P('section', 'mem', None, 'tp'), may hold values from -250 to 250
- value_cache: bfloat16 [2, 32, 4096, 1024], P('section', 'mem', None, 'tp'), may hold values from -12 to 12
Outputs:
- layer_outputs: bfloat16 [2, 32, 8192], P('section', None, 'mem')
Inputs may be any that keep to these rules, and one draw needn't show every extreme that they name: Request r has lengths[r] filled positions in its cache; the largest length is exactly 4096. Cache slot j holds request owner_order[j]; index m of mem holds slots m * 2 to (m + 1) * 2 - 1.
All inputs are finite; a program needn't handle non-finite values.
Results may differ from a plain program's by a relative error of at most 0.014.
Values may be sent and summed in bfloat16 or wider, within the bound.
A program may use at most 64 MiB of HBM per device.

v0:
```python
import math

import jax
import jax.numpy as jnp
from jax import lax
from jax.sharding import PartitionSpec as P

D = 8192
HD = 128


epsilon = 1e-05
rope_base = 500000.0


def sent_to_all(value, axis):
    count = lax.axis_size(axis)
    return lax.all_to_all(
        jnp.broadcast_to(value[None], (count, *value.shape)), axis, 0, 0, tiled=True
    )


def taken_together(value, axis):
    return sent_to_all(value, axis).sum(axis=0)


def split_up(value, dim, count):
    before, after = (value.shape[:dim], value.shape[dim + 1 :])
    return jnp.moveaxis(value.reshape(*before, count, -1, *after), dim, 0)


def summed_on_arrival(value, axis, dim):
    count = lax.axis_size(axis)
    pieces = lax.all_to_all(split_up(value, dim, count), axis, 0, 0, tiled=True)
    return jnp.sum(pieces, axis=0)


def side_by_side(arrays, axis, dim, along):
    widths = [math.prod(a.shape[along:]) for a in arrays]
    both = jnp.concatenate(
        [a.reshape(*a.shape[:along], w) for a, w in zip(arrays, widths)], axis=along
    )
    filled = summed_on_arrival(both, axis, dim)
    pieces = jnp.split(filled, [sum(widths[:k]) for k in range(1, len(widths))], axis=along)
    return tuple(
        (b.reshape(*filled.shape[:along], *a.shape[along:]) for a, b in zip(arrays, pieces))
    )


def joined_along(pieces, dim):
    shape = list(pieces.shape[1:])
    shape[dim] *= pieces.shape[0]
    return jnp.moveaxis(pieces, 0, dim).reshape(shape)


def gather_directly(value, axis, dim):
    pieces = sent_to_all(value, axis)
    return joined_along(pieces, dim)


def from_behind(value, axis, by):
    count = lax.axis_size(axis)
    pairs = [(i, i + by) for i in range(count) if 0 <= i + by < count]
    return lax.ppermute(value, axis, pairs)


def rotate(vectors, positions):
    size = vectors.shape[-1]
    half = size // 2
    freqs = rope_base ** (-(jnp.arange(half, dtype=jnp.float32) * 2.0) / size)
    angles = positions[:, None, None] * freqs[None, None, :]
    cosine = jnp.concatenate([jnp.cos(angles), jnp.cos(angles)], axis=-1)
    sine = jnp.concatenate([jnp.sin(angles), jnp.sin(angles)], axis=-1)
    turned = jnp.concatenate([-vectors[..., half:], vectors[..., :half]], axis=-1)
    return vectors * cosine + turned * sine


def feature_sum(values):
    return taken_together(values, "tp")


def scale_rows(states, norm_gain):
    as_float = states.astype(jnp.float32)
    squares = jnp.sum(as_float * as_float, axis=1)
    scaled = (as_float * norm_gain.astype(jnp.float32)[None, :]).astype(jnp.bfloat16)
    return (scaled, squares)


def row_factor(total_squares):
    return lax.rsqrt(total_squares / D + epsilon)


def decoder_layer(
    states,
    owner_order,
    inverse_order,
    slot_lengths,
    attn_gain,
    w_query,
    w_key,
    w_value,
    w_out,
    ffn_gain,
    w_gate,
    w_up,
    w_down,
    key_rows,
    value_rows,
):
    request_count = states.shape[0]
    slot_count = request_count // lax.axis_size("mem")
    query_cols = w_query.shape[1]
    kv_cols = w_key.shape[1]
    kv_heads = kv_cols // HD
    group_size = query_cols // kv_cols
    scaled, squares = scale_rows(states, attn_gain)
    scaled_slots = jnp.take(scaled, owner_order, axis=0)
    slot_squares = jnp.take(squares, owner_order, axis=0)
    rows = scaled_slots
    head_rows, own_squares = side_by_side(
        (
            jnp.concatenate(
                [
                    jnp.dot(rows, w_query, preferred_element_type=jnp.float32),
                    jnp.dot(rows, w_key, preferred_element_type=jnp.float32),
                    jnp.dot(rows, w_value, preferred_element_type=jnp.float32),
                ],
                axis=1,
            ),
            slot_squares,
        ),
        "mem",
        0,
        1,
    )
    slot_factor = row_factor(own_squares)
    head_rows = head_rows * slot_factor[:, None]
    positions = slot_lengths.astype(jnp.float32)
    queries = rotate(head_rows[:, :query_cols].reshape(slot_count, -1, HD), positions).astype(
        jnp.bfloat16
    )
    new_keys = rotate(
        head_rows[:, query_cols : query_cols + kv_cols].reshape(slot_count, kv_heads, HD), positions
    ).astype(jnp.bfloat16)
    new_values = (
        head_rows[:, query_cols + kv_cols :].reshape(slot_count, kv_heads, HD).astype(jnp.bfloat16)
    )
    context = key_rows.shape[1]
    keys_here = key_rows.reshape(slot_count, context, kv_heads, HD)
    values_here = value_rows.reshape(slot_count, context, kv_heads, HD)
    grouped = queries.reshape(slot_count, kv_heads, group_size, HD)
    score_scale = 1.0 / math.sqrt(HD)
    scores = (
        jnp.einsum("sgrd,sjgd->sgrj", grouped, keys_here, preferred_element_type=jnp.float32)
        * score_scale
    )
    live_slots = jnp.arange(context, dtype=jnp.int32)[None, :] < slot_lengths[:, None]
    scores = jnp.where(live_slots[:, None, None, :], scores, -jnp.inf)
    own_score = (
        jnp.einsum("sgrd,sgd->sgr", grouped, new_keys, preferred_element_type=jnp.float32)
        * score_scale
    )
    peak_score = jnp.maximum(jnp.max(scores, axis=-1), own_score)
    soft_weights = jnp.exp(scores - peak_score[..., None])
    own_weight = jnp.exp(own_score - peak_score)
    softmax_total = jnp.sum(soft_weights, axis=-1) + own_weight
    own_rounded = lax.optimization_barrier(own_weight.astype(jnp.bfloat16)).astype(jnp.float32)
    mixed_heads = jnp.einsum(
        "sgrj,sjgd->sgrd",
        soft_weights.astype(jnp.bfloat16),
        values_here,
        preferred_element_type=jnp.float32,
    )
    mixed_heads = (
        mixed_heads + own_rounded[..., None] * new_values.astype(jnp.float32)[:, :, None, :]
    )
    attended = (
        (mixed_heads / softmax_total[..., None])
        .astype(jnp.bfloat16)
        .reshape(slot_count, query_cols)
    )
    projected = jnp.dot(
        gather_directly(attended, "mem", 0), w_out, preferred_element_type=jnp.float32
    )
    attention_out = feature_sum(jnp.take(projected, inverse_order, axis=0))
    after_attention = (states.astype(jnp.float32) + attention_out).astype(jnp.bfloat16)
    scaled_second, squares_second = scale_rows(after_attention, ffn_gain)
    unit_count = w_gate.shape[1]
    rows = scaled_second
    own_units, own_squares_second = side_by_side(
        (
            jnp.concatenate(
                [
                    jnp.dot(rows, w_gate, preferred_element_type=jnp.float32),
                    jnp.dot(rows, w_up, preferred_element_type=jnp.float32),
                ],
                axis=1,
            ),
            squares_second,
        ),
        "mem",
        0,
        1,
    )
    own_factor = row_factor(own_squares_second)
    own_units = own_units * own_factor[:, None]
    hidden_rows = (jax.nn.silu(own_units[:, :unit_count]) * own_units[:, unit_count:]).astype(
        jnp.bfloat16
    )
    down_terms = jnp.dot(
        gather_directly(hidden_rows, "mem", 0), w_down, preferred_element_type=jnp.float32
    )
    feed_out = feature_sum(down_terms)
    return (after_attention.astype(jnp.float32) + feed_out).astype(jnp.bfloat16)


def per_device(
    hidden_in,
    lengths,
    owner_order,
    attn_gain,
    w_query,
    w_key,
    w_value,
    w_out,
    ffn_gain,
    w_gate,
    w_up,
    w_down,
    key_cache,
    value_cache,
):
    slot_count = hidden_in.shape[0] // lax.axis_size("mem")
    inverse_order = jnp.argsort(owner_order)
    slot_requests = lax.dynamic_slice_in_dim(
        owner_order, lax.axis_index("mem") * slot_count, slot_count, 0
    )
    slot_lengths = jnp.take(lengths, slot_requests, axis=0)
    first_pass = decoder_layer(
        hidden_in,
        owner_order,
        inverse_order,
        slot_lengths,
        attn_gain[0],
        w_query[0],
        w_key[0],
        w_value[0],
        w_out[0],
        ffn_gain[0],
        w_gate[0],
        w_up[0],
        w_down[0],
        key_cache[0],
        value_cache[0],
    )
    passed = from_behind(first_pass, "section", 1)
    second_pass = decoder_layer(
        passed,
        owner_order,
        inverse_order,
        slot_lengths,
        attn_gain[0],
        w_query[0],
        w_key[0],
        w_value[0],
        w_out[0],
        ffn_gain[0],
        w_gate[0],
        w_up[0],
        w_down[0],
        key_cache[0],
        value_cache[0],
    )
    result = jnp.where(lax.axis_index("section") == 0, first_pass, second_pass)
    return result[None]


def solution(mesh):
    placed = (
        P(None, "mem"),
        P(),
        P(),
        P("section", "mem"),
        P("section", "mem", "tp"),
        P("section", "mem", "tp"),
        P("section", "mem", "tp"),
        P("section", "tp", "mem"),
        P("section", "mem"),
        P("section", "mem", "tp"),
        P("section", "mem", "tp"),
        P("section", "tp", "mem"),
        P("section", "mem", None, "tp"),
        P("section", "mem", None, "tp"),
    )
    return jax.shard_map(
        per_device, mesh=mesh, in_specs=placed, out_specs=P("section", None, "mem"), check_vma=False
    )
```

profile of v0, /device:TPU:2, one launch (start us, length us, event | category | flops | bytes accessed | tf_op | source)
XLA Modules:
  0.0 206.9 jit_solution(1334204298453916275)
XLA Ops:
  0.0 0.8 compare_select_fusion.1
  1.5 0.9 fusion.68
  4.8 1.1 fusion.64
  5.9 1.0 fusion.60
  6.9 1.5 fusion.50
  9.2 7.5 %all-to-all-start = ((f32[16,2,1281]{2,1,0:T(2,128)}), f32[16,2,1281]{2,1,0:T(2,128)S(1)}, u32[]{:S(2)}, u32[]{:S(2)}) async-start(f32[16,2,1281]{2,1,0:T(2,128)} %copy.65), calls=%async_computation | async-start | bytes 360448 | tf_op jit(solution)/shard_map/all_to_all | solution.py:34
  17.8 1.6 sort.17
  19.6 4.0 %all-to-all-done = f32[16,2,1281]{2,1,0:T(2,128)S(1)} async-done(((f32[16,2,1281]{2,1,0:T(2,128)}), f32[16,2,1281]{2,1,0:T(2,128)S(1)}, u32[]{:S(2)}, u32[]{:S(2)}) %all-to-all-start) | async-done | bytes 164000 | tf_op jit(solution)/shard_map/all_to_all | solution.py:34
  26.4 4.7 %all-to-all-start.1 = ((bf16[16,2,1024]{2,1,0:T(2,128)(2,1)}), bf16[16,2,1024]{2,1,0:T(2,128)(2,1)S(1)}, u32[]{:S(2)}, u32[]{:S(2)}) async-start(bf16[16,2,1024]{2,1,0:T(2,128)(2,1)} %broadcast_in_dim.70), calls=%async_computation.1 | async-start | bytes 131072 | tf_op jit(solution)/shard_map/all_to_all | solution.py:18
  31.2 6.3 %all-to-all-done.1 = bf16[16,2,1024]{2,1,0:T(2,128)(2,1)S(1)} async-done(((bf16[16,2,1024]{2,1,0:T(2,128)(2,1)}), bf16[16,2,1024]{2,1,0:T(2,128)(2,1)S(1)}, u32[]{:S(2)}, u32[]{:S(2)}) %all-to-all-start.1) | async-done | bytes 65568 | tf_op jit(solution)/shard_map/all_to_all | solution.py:18
  38.5 0.9 broadcast_in_dim.71
  39.4 8.5 %all-to-all-start.2 = ((f32[8,32,512]{2,1,0:T(8,128)}), f32[8,32,512]{2,1,0:T(8,128)S(1)}, u32[]{:S(2)}, u32[]{:S(2)}) async-start(f32[8,32,512]{2,1,0:T(8,128)} %broadcast_in_dim.71), calls=%async_computation.2 | async-start | bytes 1048576 | tf_op jit(solution)/shard_map/all_to_all | solution.py:18
  47.9 14.9 %all-to-all-done.2 = f32[8,32,512]{2,1,0:T(8,128)S(1)} async-done(((f32[8,32,512]{2,1,0:T(8,128)}), f32[8,32,512]{2,1,0:T(8,128)S(1)}, u32[]{:S(2)}, u32[]{:S(2)}) %all-to-all-start.2) | async-done | bytes 524320 | tf_op jit(solution)/shard_map/all_to_all | solution.py:18
  63.3 2.1 fusion.14
  66.1 13.3 %all_to_all.60 = f32[16,2,3585]{2,1,0:T(2,128)S(1)} all-to-all(f32[16,2,3585]{2,1,0:T(2,128)S(1)} %copy.69), channel_id=1, replica_groups=mesh['section'=2,'tp'=8,'mem'=16] {'mem'}, dimensions={0} | all-to-all | bytes 917760 | tf_op jit(solution)/shard_map/all_to_all | solution.py:34
  79.8 10.9 %all_to_all.61 = bf16[16,2,1792]{2,1,0:T(2,128)(2,1)S(1)} all-to-all(bf16[16,2,1792]{2,1,0:T(2,128)(2,1)S(1)} %broadcast_in_dim.72), channel_id=1, replica_groups=mesh['section'=2,'tp'=8,'mem'=16] {'mem'}, dimensions={0} | all-to-all | bytes 229376 | tf_op jit(solution)/shard_map/all_to_all | solution.py:18
  90.7 1.9 fusion.10
  92.7 16.5 %all_to_all.62 = f32[8,32,512]{2,1,0:T(8,128)} all-to-all(f32[8,32,512]{2,1,0:T(8,128)S(1)} %broadcast_in_dim.73), channel_id=1, replica_groups=mesh['section'=2,'tp'=8,'mem'=16] {'tp'}, dimensions={0} | all-to-all | bytes 1048576 | tf_op jit(solution)/shard_map/all_to_all | solution.py:18
  109.2 1.1 reduce_sum.132
  110.3 1.3 collective-permute-start
  111.6 0.8 collective-permute-done
  113.9 0.8 gather_fusion.5
  115.2 11.4 %all_to_all.63 = f32[16,2,1281]{2,1,0:T(2,128)S(1)} all-to-all(f32[16,2,1281]{2,1,0:T(2,128)S(1)} %copy.74), channel_id=1, replica_groups=mesh['section'=2,'tp'=8,'mem'=16] {'mem'}, dimensions={0} | all-to-all | bytes 327936 | tf_op jit(solution)/shard_map/all_to_all | solution.py:34
  128.9 10.7 %all_to_all.64 = bf16[16,2,1024]{2,1,0:T(2,128)(2,1)S(1)} all-to-all(bf16[16,2,1024]{2,1,0:T(2,128)(2,1)S(1)} %broadcast_in_dim.75), channel_id=1, replica_groups=mesh['section'=2,'tp'=8,'mem'=16] {'mem'}, dimensions={0} | all-to-all | bytes 131072 | tf_op jit(solution)/shard_map/all_to_all | solution.py:18
  140.7 18.1 %all_to_all.65 = f32[8,32,512]{2,1,0:T(8,128)S(1)} all-to-all(f32[8,32,512]{2,1,0:T(8,128)S(1)} %broadcast_in_dim.76), channel_id=1, replica_groups=mesh['section'=2,'tp'=8,'mem'=16] {'tp'}, dimensions={0} | all-to-all | bytes 1048576 | tf_op jit(solution)/shard_map/all_to_all | solution.py:18
  158.9 2.0 fusion.12
  162.1 13.3 %all_to_all.66 = f32[16,2,3585]{2,1,0:T(2,128)S(1)} all-to-all(f32[16,2,3585]{2,1,0:T(2,128)S(1)} %copy.78), channel_id=1, replica_groups=mesh['section'=2,'tp'=8,'mem'=16] {'mem'}, dimensions={0} | all-to-all | bytes 917760 | tf_op jit(solution)/shard_map/all_to_all | solution.py:34
  175.8 10.9 %all_to_all.67 = bf16[16,2,1792]{2,1,0:T(2,128)(2,1)S(1)} all-to-all(bf16[16,2,1792]{2,1,0:T(2,128)(2,1)S(1)} %broadcast_in_dim.77), channel_id=1, replica_groups=mesh['section'=2,'tp'=8,'mem'=16] {'mem'}, dimensions={0} | all-to-all | bytes 229376 | tf_op jit(solution)/shard_map/all_to_all | solution.py:18
  186.7 1.9 fusion.8
  188.6 0.9 broadcast_in_dim.78
  189.5 3.5 %all-to-all-start.11 = ((f32[8,32,512]{2,1,0:T(8,128)}), f32[8,32,512]{2,1,0:T(8,128)S(1)}, u32[]{:S(2)}, u32[]{:S(2)}) async-start(f32[8,32,512]{2,1,0:T(8,128)} %broadcast_in_dim.78), calls=%async_computation.11 | async-start | bytes 1048576 | tf_op jit(solution)/shard_map/all_to_all | solution.py:18
  193.0 13.2 %all-to-all-done.11 = f32[8,32,512]{2,1,0:T(8,128)S(1)} async-done(((f32[8,32,512]{2,1,0:T(8,128)}), f32[8,32,512]{2,1,0:T(8,128)S(1)}, u32[]{:S(2)}, u32[]{:S(2)}) %all-to-all-start.11) | async-done | bytes 524320 | tf_op jit(solution)/shard_map/all_to_all | solution.py:18
  (172 shorter events, 18.2 us)
Async XLA Ops:
  0.0 24.3 %copy-start = (bf16[1,2,4096,128]{3,2,1,0:T(8,128)(2,1)S(1)}, bf16[1,2,4096,128]{3,2,1,0:T(8,128)(2,1)}, u32[]{:S(2)}) copy-start(bf16[1,2,4096,128]{3,2,1,0:T(8,128)(2,1)} %param.32) | copy-start | bytes 6291460
  1.5 111.1 %copy-start.18 = (s32[1024]{0:T(1024)}, s32[1024]{0:T(1024)S(1)}, u32[]{:S(2)}) copy-start(s32[1024]{0:T(1024)S(1)} %pad_clamp_fusion.1) | copy-start | bytes 12292
  2.4 14.3 %copy-start.25 = (s32[32]{0:T(128)S(1)}, s32[32]{0:T(128)}, u32[]{:S(2)}) copy-start(s32[32]{0:T(128)} %param.22) | copy-start | bytes 388
  2.4 14.4 %copy-start.1 = (s32[32]{0:T(128)S(1)}, s32[32]{0:T(128)}, u32[]{:S(2)}) copy-start(s32[32]{0:T(128)} %param.21) | copy-start | bytes 388
  4.4 108.8 %copy-start.20 = (pred[32]{0:T(512)(128)(4,1)}, pred[32]{0:T(512)(128)(4,1)S(1)}, u32[]{:S(2)}) copy-start(pred[32]{0:T(512)(128)(4,1)S(1)} %get-tuple-element.17) | copy-start | bytes 100
  9.2 14.4 %all-to-all-start = ((f32[16,2,1281]{2,1,0:T(2,128)}), f32[16,2,1281]{2,1,0:T(2,128)S(1)}, u32[]{:S(2)}, u32[]{:S(2)}) async-start(f32[16,2,1281]{2,1,0:T(2,128)} %copy.65), calls=%async_computation | async-start | bytes 360448 | tf_op jit(solution)/shard_map/all_to_all | solution.py:34
  17.6 6.7 %copy-start.14 = (f32[2,64]{1,0:T(2,128)}, f32[2,64]{1,0:T(2,128)S(1)}, u32[]{:S(2)}) copy-start(f32[2,64]{1,0:T(2,128)S(1)} %get-tuple-element.32) | copy-start | bytes 1540
  17.6 8.1 %copy-start.16 = (f32[2,64]{1,0:T(2,128)}, f32[2,64]{1,0:T(2,128)S(1)}, u32[]{:S(2)}) copy-start(f32[2,64]{1,0:T(2,128)S(1)} %get-tuple-element.33) | copy-start | bytes 1540
  19.4 19.1 %copy-start.22 = (pred[32]{0:T(512)(128)(4,1)}, pred[32]{0:T(512)(128)(4,1)S(1)}, u32[]{:S(2)}) copy-start(pred[32]{0:T(512)(128)(4,1)S(1)} %compare_and_fusion) | copy-start | bytes 100
  23.6 1.6 copy-start.2
  25.0 12.5 %copy-start.7 = (bf16[1,1024,512]{2,1,0:T(8,128)(2,1)S(1)}, bf16[1,1024,512]{2,1,0:T(8,128)(2,1)}, u32[]{:S(2)}) copy-start(bf16[1,1024,512]{2,1,0:T(8,128)(2,1)} %param.27) | copy-start | bytes 3145732
  26.4 11.1 %all-to-all-start.1 = ((bf16[16,2,1024]{2,1,0:T(2,128)(2,1)}), bf16[16,2,1024]{2,1,0:T(2,128)(2,1)S(1)}, u32[]{:S(2)}, u32[]{:S(2)}) async-start(bf16[16,2,1024]{2,1,0:T(2,128)(2,1)} %broadcast_in_dim.70), calls=%async_computation.1 | async-start | bytes 131072 | tf_op jit(solution)/shard_map/all_to_all | solution.py:18
  31.1 8.2 %copy-start.19 = (s32[1024]{0:T(1024)}, s32[1024]{0:T(1024)S(1)}, u32[]{:S(2)}) copy-start(s32[1024]{0:T(1024)S(1)} %pad_clamp_fusion) | copy-start | bytes 12292
  31.2 16.7 %copy-start.24 = (bf16[1,512]{1,0:T(2,128)(2,1)S(1)}, bf16[1,512]{1,0:T(2,128)(2,1)}, u32[]{:S(2)}) copy-start(bf16[1,512]{1,0:T(2,128)(2,1)} %param.28) | copy-start | bytes 3076
  37.5 25.3 %copy-start.13 = (bf16[32,512]{1,0:T(8,128)(2,1)S(1)}, bf16[32,512]{1,0:T(8,128)(2,1)}, u32[]{:S(2)}) copy-start(bf16[32,512]{1,0:T(8,128)(2,1)} %param.20) | copy-start | bytes 98308
  39.4 23.4 %all-to-all-start.2 = ((f32[8,32,512]{2,1,0:T(8,128)}), f32[8,32,512]{2,1,0:T(8,128)S(1)}, u32[]{:S(2)}, u32[]{:S(2)}) async-start(f32[8,32,512]{2,1,0:T(8,128)} %broadcast_in_dim.71), calls=%async_computation.2 | async-start | bytes 1048576 | tf_op jit(solution)/shard_map/all_to_all | solution.py:18
  63.3 2.1 copy-start.4
  92.6 20.7 %copy-start.9 = (bf16[1,512,128]{2,1,0:T(8,128)(2,1)S(1)}, bf16[1,512,128]{2,1,0:T(8,128)(2,1)}, u32[]{:S(2)}) copy-start(bf16[1,512,128]{2,1,0:T(8,128)(2,1)} %param.25) | copy-start | bytes 393220
  92.6 20.9 %copy-start.10 = (bf16[1,512,128]{2,1,0:T(8,128)(2,1)S(1)}, bf16[1,512,128]{2,1,0:T(8,128)(2,1)}, u32[]{:S(2)}) copy-start(bf16[1,512,128]{2,1,0:T(8,128)(2,1)} %param.26) | copy-start | bytes 393220
  92.7 21.0 %copy-start.6 = (bf16[1,512,1024]{2,1,0:T(8,128)(2,1)S(1)}, bf16[1,512,1024]{2,1,0:T(8,128)(2,1)}, u32[]{:S(2)}) copy-start(bf16[1,512,1024]{2,1,0:T(8,128)(2,1)} %param.24) | copy-start | bytes 3145732
  110.3 2.3 %copy-start.11 = (bf16[32,512]{1,0:T(8,128)(2,1)}, bf16[32,512]{1,0:T(8,128)(2,1)S(1)}, u32[]{:S(2)}) copy-start(bf16[32,512]{1,0:T(8,128)(2,1)S(1)} %fusion.73) | copy-start | bytes 98308
  110.3 2.1 %collective-permute-start = (bf16[32,512]{1,0:T(8,128)(2,1)S(1)}, bf16[32,512]{1,0:T(8,128)(2,1)S(1)}, u32[]{:S(2)}, u32[]{:S(2)}) collective-permute-start(bf16[32,512]{1,0:T(8,128)(2,1)S(1)} %fusion.73), channel_id=1, source_target_pairs={{0,128},{1,129},{2,130},{3,131},{4,132},{5,133},{6,134},{7,135},{8... | collective-permute-start | bytes 98312 | tf_op jit(solution)/shard_map/ppermute | solution.py:64
  113.5 1.3 copy-start.21
  115.1 12.8 %copy-start.15 = (f32[2,64]{1,0:T(2,128)S(1)}, f32[2,64]{1,0:T(2,128)}, u32[]{:S(2)}) copy-start(f32[2,64]{1,0:T(2,128)} %copy-done.14) | copy-start | bytes 1540
  115.1 12.8 %copy-start.17 = (f32[2,64]{1,0:T(2,128)S(1)}, f32[2,64]{1,0:T(2,128)}, u32[]{:S(2)}) copy-start(f32[2,64]{1,0:T(2,128)} %copy-done.16) | copy-start | bytes 1540
  126.7 1.6 copy-start.3
  127.9 11.7 %copy-start.8 = (bf16[1,1024,512]{2,1,0:T(8,128)(2,1)S(1)}, bf16[1,1024,512]{2,1,0:T(8,128)(2,1)}, u32[]{:S(2)}) copy-start(bf16[1,1024,512]{2,1,0:T(8,128)(2,1)} %param.27) | copy-start | bytes 3145732
  128.3 12.3 %copy-start.23 = (pred[32]{0:T(512)(128)(4,1)S(1)}, pred[32]{0:T(512)(128)(4,1)}, u32[]{:S(2)}) copy-start(pred[32]{0:T(512)(128)(4,1)} %copy-done.22) | copy-start | bytes 100
  158.9 2.1 copy-start.5
  186.7 19.5 %copy-start.12 = (bf16[32,512]{1,0:T(8,128)(2,1)S(1)}, bf16[32,512]{1,0:T(8,128)(2,1)}, u32[]{:S(2)}) copy-start(bf16[32,512]{1,0:T(8,128)(2,1)} %copy-done.11) | copy-start | bytes 98308
  189.5 16.7 %all-to-all-start.11 = ((f32[8,32,512]{2,1,0:T(8,128)}), f32[8,32,512]{2,1,0:T(8,128)S(1)}, u32[]{:S(2)}, u32[]{:S(2)}) async-start(f32[8,32,512]{2,1,0:T(8,128)} %broadcast_in_dim.78), calls=%async_computation.11 | async-start | bytes 1048576 | tf_op jit(solution)/shard_map/all_to_all | solution.py:18
where the time goes:
time: 208 us; the launch traced here: 207 us
  blocking collectives  105 us (50%)
  waiting for transfers between devices  39.3 us (19%)
  starting transfers between devices  25.5 us (12%)
  matrix products  16.1 us (8%)
  local copies, waits for them, and re-layouts  10.3 us (5%)
  other arithmetic  10.3 us (5%)
    all_to_all x5, blocking collectives, sent_to_all(): lax.all_to_all(jnp.broadcast_to(value[None], (count, *value.shape)), axis...  67 us
    all_to_all x3, blocking collectives, summed_on_arrival(): pieces = lax.all_to_all(split_up(value, dim, count), axis, 0, 0, tiled=True)  38 us
    all_to_all x3, waiting for transfers between devices, sent_to_all(): lax.all_to_all(jnp.broadcast_to(value[None], (count, *value.shape)), axis...  34.4 us
    all_to_all x3, starting transfers between devices, sent_to_all(): lax.all_to_all(jnp.broadcast_to(value[None], (count, *value.shape)), axis...  16.7 us
    all_to_all x1, starting transfers between devices, summed_on_arrival(): pieces = lax.all_to_all(split_up(value, dim, count), axis, 0, 0, tiled=True)  7.48 us
  transfers between devices with their start and end apart: 5, of which 5 were waited for; matrix products, arithmetic and copies ran while one was open for 1% of the time, Pallas kernels for 0%

commit v1 on v0

v1 whole, which is shorter than its diff:
```python
import functools
import math

import jax
import jax.numpy as jnp
import numpy as np
from jax import lax
from jax.experimental import pallas as pl
from jax.experimental.pallas import tpu as pltpu
from jax.sharding import PartitionSpec as P

D = 8192
HD = 128
CTX = 4096
ROWS = 32
EPS = 1e-05
MESH = pl.DeviceIdType.MESH
F32 = jnp.float32
BF16 = jnp.bfloat16


def _hops(o):
    return min(o[0], 4 - o[0]) + min(o[1], 4 - o[1])


OFFSETS = sorted(
    [(a, b) for a in range(4) for b in range(4) if (a, b) != (0, 0)], key=lambda o: -_hops(o)
)
RING = (4, 3, 5, 2, 6, 1, 7)
OWNERS = 14


def _nt(a, b):
    return lax.dot_general(a, b, (((1,), (1,)), ((), ())), preferred_element_type=F32)


def _nn(a, b):
    return jnp.dot(a, b, preferred_element_type=F32)


def kernel(
    lengths,
    owner,
    freqs,
    hidden_in,
    attn_gain,
    ffn_gain,
    w_query,
    w_key,
    w_value,
    w_out,
    w_gate,
    w_up,
    w_down,
    key_cache,
    value_cache,
    out,
    wqkv,
    wo,
    wg,
    wu,
    wd,
    kbuf,
    vbuf,
    xin,
    xout,
    sb1,
    rb1,
    sb2,
    rb2,
    fb2,
    sb3,
    rb3,
    ssq,
    rsq,
    sb4,
    rb4,
    sb5,
    rb5,
    sb6,
    rb6,
    wsem,
    send,
    recv,
):
    sec = lax.axis_index("section")
    tp = lax.axis_index("tp")
    mem = lax.axis_index("mem")
    my, mx = mem // 4, lax.rem(mem, 4)

    def peer(o):
        return lax.rem(my + o[0], 4) * 4 + lax.rem(mx + o[1], 4)

    def slot_at(o):
        return ((4 - o[0]) % 4) * 4 + (4 - o[1]) % 4

    loads = [
        (w_query.at[0], wqkv.at[:, pl.ds(0, 1024)]),
        (w_key.at[0], wqkv.at[:, pl.ds(1024, 128)]),
        (w_value.at[0], wqkv.at[:, pl.ds(1152, 128)]),
        (key_cache.at[0, 0], kbuf.at[:, pl.ds(0, 128)]),
        (key_cache.at[0, 1], kbuf.at[:, pl.ds(128, 128)]),
        (value_cache.at[0, 0], vbuf.at[:, pl.ds(0, 128)]),
        (value_cache.at[0, 1], vbuf.at[:, pl.ds(128, 128)]),
        (w_out.at[0], wo),
        (w_gate.at[0], wg),
        (w_up.at[0], wu),
        (w_down.at[0], wd),
    ]
    loads = [pltpu.make_async_copy(s, d, wsem.at[i]) for i, (s, d) in enumerate(loads)]
    for c in loads[:3]:
        c.start()

    barrier = pltpu.get_barrier_semaphore()
    for o in OFFSETS:
        pl.semaphore_signal(barrier, inc=1, device_id={"mem": peer(o)}, device_id_type=MESH)
    for k in RING:
        pl.semaphore_signal(
            barrier, inc=1, device_id={"tp": lax.rem(tp + k, 8)}, device_id_type=MESH
        )
    pl.semaphore_signal(barrier, inc=1, device_id={"section": 1 - sec}, device_id_type=MESH)
    for c in loads[3:]:
        c.start()

    row = lax.broadcasted_iota(jnp.int32, (ROWS, ROWS), 0)
    col = lax.broadcasted_iota(jnp.int32, (ROWS, ROWS), 1)
    by_row = jnp.zeros((ROWS, ROWS), jnp.int32)
    by_col = jnp.zeros((ROWS, ROWS), jnp.int32)
    for j in range(ROWS):
        r = owner[j]
        by_row = jnp.where(row == j, r, by_row)
        by_col = jnp.where(col == j, r, by_col)
    to_slots = jnp.where(by_row == col, 1.0, 0.0).astype(BF16)
    to_requests = jnp.where(by_col == row, 1.0, 0.0).astype(BF16)

    len0 = lengths[owner[2 * mem]]
    len1 = lengths[owner[2 * mem + 1]]
    upper = lax.broadcasted_iota(jnp.int32, (8, 128), 0) < 4
    angles = jnp.where(upper, len0, len1).astype(F32) * freqs[...]
    cosine = jnp.cos(angles)
    sine = jnp.sin(angles)
    lane = lax.broadcasted_iota(jnp.int32, (8, 128), 1)
    sine = jnp.where(lane < 64, -sine, sine)

    @pl.when(sec == 0)
    def _():
        xin[...] = _nn(to_slots, hidden_in[...]).astype(BF16)

    pl.semaphore_wait(barrier, 23)

    @pl.when(sec == 1)
    def _():
        pltpu.make_async_copy(xout, xin, recv.at[7]).wait()

    x = xin[...].astype(F32)
    scaled = (x * attn_gain[...].astype(F32)).astype(BF16)
    squares = jnp.sum(x * x, axis=1, keepdims=True)
    for c in loads[:3]:
        c.wait()
    part = _nn(scaled, wqkv[...])
    for h in range(10):
        sb1[pl.ds(h, ROWS, stride=12), :] = part[:, h * 128 : (h + 1) * 128]
    sb1[pl.ds(10, ROWS, stride=12), :] = jnp.broadcast_to(squares, (ROWS, 128))
    sb1[pl.ds(11, ROWS, stride=12), :] = jnp.zeros((ROWS, 128), F32)

    def rows_of(m):
        return pl.ds(pl.multiple_of(m * 24, 8), 24)

    for o in OFFSETS:
        pltpu.make_async_remote_copy(
            src_ref=sb1.at[rows_of(peer(o))],
            dst_ref=rb1.at[slot_at(o)],
            send_sem=send.at[0],
            recv_sem=recv.at[0],
            device_id={"mem": peer(o)},
            device_id_type=MESH,
        ).start()
    heads = sb1[rows_of(mem), :]
    from15 = pl.ds(1, 15)
    pltpu.make_async_copy(rb1.at[from15], rb1.at[from15], recv.at[0]).wait()
    for k in range(1, 16):
        heads = heads + rb1[k]

    def turned(v, s):
        c, n = cosine[4 * s : 4 * s + 1], sine[4 * s : 4 * s + 1]
        return v * c + pltpu.roll(v, 64, 1) * n

    scale = 1.0 / math.sqrt(HD)
    zero = jnp.zeros((8, 128), F32)
    queries, owns, values = [], [], []
    for s in range(2):
        mine = heads[12 * s : 12 * s + 12]
        mine = mine * lax.rsqrt(mine[10:11] / D + EPS)
        q = turned(mine[0:8], s)
        kv = turned(mine[8:9], s).astype(BF16).astype(F32)
        values.append(jnp.broadcast_to(mine[9:10].astype(BF16).astype(F32), (8, 128)))
        q = q.astype(BF16).astype(F32)
        owns.append(jnp.sum(q * kv, axis=1, keepdims=True) * scale)
        queries.append(jnp.concatenate([q, zero] if s == 0 else [zero, q], axis=1))
    queries = jnp.concatenate(queries, axis=0).astype(BF16)
    own_score = jnp.concatenate(owns, axis=0)
    new_values = jnp.concatenate(values, axis=0)
    loads[3].wait()
    loads[4].wait()
    scores = _nt(queries, kbuf[...]) * scale
    where = lax.broadcasted_iota(jnp.int32, (16, CTX), 1)
    first = lax.broadcasted_iota(jnp.int32, (16, 1), 0) < 8
    scores = jnp.where(where < jnp.where(first, len0, len1), scores, -jnp.inf)
    peak = jnp.maximum(jnp.max(scores, axis=1, keepdims=True), own_score)
    soft = jnp.exp(scores - peak)
    own = jnp.exp(own_score - peak)
    total = jnp.sum(soft, axis=1, keepdims=True) + own
    loads[5].wait()
    loads[6].wait()
    mixed = _nn(soft.astype(BF16), vbuf[...])
    mixed = jnp.where(first, mixed[:, :128], mixed[:, 128:])
    mixed = mixed + own.astype(BF16).astype(F32) * new_values
    attended = (mixed / total).astype(BF16)
    sb2[...] = attended
    rb2[mem] = attended
    for o in OFFSETS:
        pltpu.make_async_remote_copy(
            src_ref=sb2,
            dst_ref=rb2.at[mem],
            send_sem=send.at[1],
            recv_sem=recv.at[1],
            device_id={"mem": peer(o)},
            device_id_type=MESH,
        ).start()
    loads[7].wait()
    pltpu.make_async_copy(rb2.at[from15], rb2.at[from15], recv.at[1]).wait()
    fb2[...] = rb2[...].astype(F32).reshape(256, 128)
    wide = jnp.concatenate([fb2[pl.ds(h, ROWS, stride=8), :] for h in range(8)], axis=1)
    part = _nn(wide.astype(BF16), wo[...])

    from7 = pl.ds(1, 7)

    def tp_sum(part, sb, rb, which):
        sb[...] = part.astype(BF16)
        for k in RING:
            pltpu.make_async_remote_copy(
                src_ref=sb,
                dst_ref=rb.at[tp],
                send_sem=send.at[which],
                recv_sem=recv.at[which],
                device_id={"tp": lax.rem(tp + k, 8)},
                device_id_type=MESH,
            ).start()
        rb[tp] = sb[...]
        pltpu.make_async_copy(rb.at[from7], rb.at[from7], recv.at[which]).wait()
        total = rb[0].astype(F32)
        for k in range(1, 8):
            total = total + rb[k].astype(F32)
        return total

    x = (x + tp_sum(part, sb3, rb3, 2)).astype(BF16).astype(F32)

    squares = jnp.sum(x * x, axis=1, keepdims=True)
    packed = jnp.zeros((8, 128), F32)
    for g in range(4):
        packed = jnp.where(lane // 32 == g, squares[8 * g : 8 * g + 8], packed)
    ssq[...] = packed
    for o in OFFSETS:
        pltpu.make_async_remote_copy(
            src_ref=ssq,
            dst_ref=rsq.at[slot_at(o)],
            send_sem=send.at[3],
            recv_sem=recv.at[3],
            device_id={"mem": peer(o)},
            device_id_type=MESH,
        ).start()
    scaled = (x * ffn_gain[...].astype(F32)).astype(BF16)
    loads[8].wait()
    loads[9].wait()

    def columns(j):
        return pl.ds(pl.multiple_of(j * 128, 128), 128)

    def units(j):
        j = jnp.minimum(j, OWNERS - 1)
        both = jnp.concatenate([wg[:, columns(j)], wu[:, columns(j)]], axis=1)
        return _nn(scaled, both)

    groups = (OFFSETS[:5], OFFSETS[5:11], OFFSETS[11:])
    for group in groups:
        for o in group:
            sb4[o[0] * 4 + o[1]] = units(peer(o)).astype(BF16)
        for o in group:

            @pl.when(peer(o) < OWNERS)
            def _(o=o):
                pltpu.make_async_remote_copy(
                    src_ref=sb4.at[o[0] * 4 + o[1]],
                    dst_ref=rb4.at[slot_at(o)],
                    send_sem=send.at[4],
                    recv_sem=recv.at[4],
                    device_id={"mem": peer(o)},
                    device_id_type=MESH,
                ).start()

    sums = units(mem)
    pltpu.make_async_copy(rsq.at[from15], rsq.at[from15], recv.at[3]).wait()
    for k in range(1, 16):
        packed = packed + rsq[k]
    packed = lax.rsqrt(packed / D + EPS)
    factor = jnp.concatenate([packed[:, 32 * g : 32 * g + 1] for g in range(4)], axis=0)

    @pl.when(mem < OWNERS)
    def _():
        pltpu.make_async_copy(rb4.at[from15], rb4.at[from15], recv.at[4]).wait()
        own_units = sums
        for k in range(1, 16):
            own_units = own_units + rb4[k].astype(F32)
        own_units = own_units * factor
        gate, up = own_units[:, :128], own_units[:, 128:]
        units_here = (gate / (1.0 + jnp.exp(-gate)) * up).astype(BF16)
        sb5[...] = units_here
        rb5[mem] = units_here
        for o in OFFSETS:
            pltpu.make_async_remote_copy(
                src_ref=sb5,
                dst_ref=rb5.at[mem],
                send_sem=send.at[5],
                recv_sem=recv.at[5],
                device_id={"mem": peer(o)},
                device_id_type=MESH,
            ).start()
        from13 = pl.ds(0, 13)
        pltpu.make_async_copy(rb5.at[from13], rb5.at[from13], recv.at[5]).wait()

    @pl.when(mem >= OWNERS)
    def _():
        from14 = pl.ds(0, 14)
        pltpu.make_async_copy(rb5.at[from14], rb5.at[from14], recv.at[5]).wait()

    loads[10].wait()
    hidden = jnp.concatenate([rb5[j] for j in range(OWNERS)], axis=1)
    part = _nn(hidden, wd[...])
    x = (x + tp_sum(part, sb6, rb6, 6)).astype(BF16)
    xout[...] = x

    across = pltpu.make_async_remote_copy(
        src_ref=xout,
        dst_ref=xin,
        send_sem=send.at[7],
        recv_sem=recv.at[7],
        device_id={"section": 1 - sec},
        device_id_type=MESH,
    )

    @pl.when(sec == 0)
    def _():
        across.start()

    out[0] = _nn(to_requests, x).astype(BF16)

    pltpu.make_async_copy(rb1.at[from15], rb1.at[from15], send.at[0]).wait()
    pltpu.make_async_copy(rb2.at[from15], rb2.at[from15], send.at[1]).wait()
    pltpu.make_async_copy(rb3.at[from7], rb3.at[from7], send.at[2]).wait()
    pltpu.make_async_copy(rsq.at[from15], rsq.at[from15], send.at[3]).wait()
    pltpu.make_async_copy(rb6.at[from7], rb6.at[from7], send.at[6]).wait()

    @pl.when(mem < OWNERS)
    def _():
        from13 = pl.ds(0, 13)
        pltpu.make_async_copy(rb4.at[from13], rb4.at[from13], send.at[4]).wait()
        all15 = pl.ds(0, 15)
        pltpu.make_async_copy(rb5.at[all15], rb5.at[all15], send.at[5]).wait()

    @pl.when(mem >= OWNERS)
    def _():
        from14 = pl.ds(0, 14)
        pltpu.make_async_copy(rb4.at[from14], rb4.at[from14], send.at[4]).wait()

    @pl.when(sec == 0)
    def _():
        across.wait_send()


FREQS = (500000.0 ** (-(np.arange(64, dtype=np.float64) * 2.0) / 128)).astype(np.float32)
FREQS = np.concatenate([FREQS, FREQS])[None, :]


def per_device(hidden_in, lengths, owner_order, attn_gain, w_query, w_key, w_value, w_out,
               ffn_gain, w_gate, w_up, w_down, key_cache, value_cache):
    smem = pl.BlockSpec(memory_space=pltpu.SMEM)
    vmem = pl.BlockSpec(memory_space=pltpu.VMEM)
    hbm = pl.BlockSpec(memory_space=pl.ANY)
    V = pltpu.VMEM
    return pl.pallas_call(
        kernel,
        out_shape=jax.ShapeDtypeStruct((1, ROWS, 512), BF16),
        in_specs=[smem, smem, vmem, vmem, vmem, vmem] + [hbm] * 9,
        out_specs=vmem,
        scratch_shapes=[
            V((512, 1280), BF16),
            V((1024, 512), BF16),
            V((512, 1792), BF16),
            V((512, 1792), BF16),
            V((1792, 512), BF16),
            V((CTX, 256), BF16),
            V((CTX, 256), BF16),
            V((ROWS, 512), BF16),
            V((ROWS, 512), BF16),
            V((384, 128), F32),
            V((16, 24, 128), F32),
            V((16, 128), BF16),
            V((16, 16, 128), BF16),
            V((256, 128), F32),
            V((ROWS, 512), BF16),
            V((8, ROWS, 512), BF16),
            V((8, 128), F32),
            V((16, 8, 128), F32),
            V((16, ROWS, 256), BF16),
            V((16, ROWS, 256), BF16),
            V((ROWS, 128), BF16),
            V((16, ROWS, 128), BF16),
            V((ROWS, 512), BF16),
            V((8, ROWS, 512), BF16),
            pltpu.SemaphoreType.DMA((11,)),
            pltpu.SemaphoreType.DMA((8,)),
            pltpu.SemaphoreType.DMA((8,)),
        ],
        compiler_params=pltpu.CompilerParams(
            collective_id=0, has_side_effects=True, vmem_limit_bytes=56 << 20
        ),
    )(
        lengths, owner_order, jnp.asarray(FREQS), hidden_in, attn_gain, ffn_gain,
        w_query, w_key, w_value, w_out, w_gate, w_up, w_down, key_cache, value_cache,
    )


def solution(mesh):
    placed = (
        P(None, "mem"),
        P(),
        P(),
        P("section", "mem"),
        P("section", "mem", "tp"),
        P("section", "mem", "tp"),
        P("section", "mem", "tp"),
        P("section", "tp", "mem"),
        P("section", "mem"),
        P("section", "mem", "tp"),
        P("section", "mem", "tp"),
        P("section", "tp", "mem"),
        P("section", "mem", None, "tp"),
        P("section", "mem", None, "tp"),
    )
    return jax.shard_map(
        per_device, mesh=mesh, in_specs=placed, out_specs=P("section", None, "mem"), check_vma=False
    )
```

time: 208 us -> 79.5 us (0.38)
  the two profiles are of different devices: /device:TPU:2 before, /device:TPU:1 now
where the time goes in v1:
time: 79.5 us; the launch traced here: 79.3 us
  Pallas kernels  77.9 us (98%)
  local copies, waits for them, and re-layouts  1.38 us (2%)
    pallas_call x1, Pallas kernels, per_device(): pl.pallas_call(kernel, out_shape=jax.ShapeDtypeStruct((1, ROWS, 512), BF1...  77.9 us

profile of v1, /device:TPU:1, one launch (start us, length us, event | category | flops | bytes accessed | tf_op | source)
XLA Modules:
  0.0 79.3 jit_solution(11936732842090515423)
XLA Ops:
  0.0 77.9 %shard_map.145 = bf16[1,32,512]{2,1,0:T(8,128)(2,1)} custom-call(s32[32]{0:T(128)} %lengths.1, s32[32]{0:T(128)} %owner.1, f32[1,128]{1,0:T(1,128)} %constant.2.clone.freqs, bf16[32,512]{1,0:T(8,128)(2,1)} %hidden_in.1, bf16[1,512]{1,0:T(2,128)(2,1)} %attn_gain.1, bf16[1,512]{1,0:T(2,128)(2,1)} %ffn_gain.1, bf16[1,512,1024]{2,1,0:T(8,128)(2,1)} %w_query.1, ...), custom_call_target="tpu_custom_call" | custom-call | tf_op jit(solution)/shard_map/pallas_call | solution.py:390
  78.0 1.4 %copy.17 = bf16[1,32,512]{2,1,0:T(8,128)(2,1)} copy(bf16[1,32,512]{2,1,0:T(8,128)(2,1)} %shard_map.145) | data formatting | bytes 65536

commit v2 on v1

--- a/solution.py
+++ b/solution.py
@@ -27,6 +27,7 @@
     [(a, b) for a in range(4) for b in range(4) if (a, b) != (0, 0)], key=lambda o: -_hops(o)
 )
 RING = (4, 3, 5, 2, 6, 1, 7)
+BARRIER = 15 + 7 + 8
 OWNERS = 14
 
 
@@ -39,12 +40,12 @@
 
 
 def kernel(
-    lengths,
-    owner,
-    freqs,
+    lengths_in,
+    owner_in,
+    freqs_in,
     hidden_in,
-    attn_gain,
-    ffn_gain,
+    attn_gain_in,
+    ffn_gain_in,
     w_query,
     w_key,
     w_value,
@@ -55,6 +56,12 @@
     key_cache,
     value_cache,
     out,
+    lengths,
+    owner,
+    freqs,
+    hidden,
+    attn_gain,
+    ffn_gain,
     wqkv,
     wo,
     wg,
@@ -64,6 +71,8 @@
     vbuf,
     xin,
     xout,
+    x2,
+    x2in,
     sb1,
     rb1,
     sb2,
@@ -79,9 +88,13 @@
     rb5,
     sb6,
     rb6,
+    ssem,
     wsem,
     send,
     recv,
+    recv4,
+    recv5,
+    recv6,
 ):
     sec = lax.axis_index("section")
     tp = lax.axis_index("tp")
@@ -94,6 +107,33 @@
     def slot_at(o):
         return ((4 - o[0]) % 4) * 4 + (4 - o[1]) % 4
 
+    barrier = pltpu.get_barrier_semaphore()
+    for k in RING:
+        pl.semaphore_signal(
+            barrier, inc=1, device_id={"tp": lax.rem(tp + k, 8)}, device_id_type=MESH
+        )
+    for o in OFFSETS:
+        pl.semaphore_signal(barrier, inc=1, device_id={"mem": peer(o)}, device_id_type=MESH)
+    pl.semaphore_signal(barrier, inc=1, device_id={"section": 1 - sec}, device_id_type=MESH)
+    for k in RING:
+        pl.semaphore_signal(
+            barrier,
+            inc=1,
+            device_id={"section": 1 - sec, "tp": lax.rem(tp + k, 8)},
+            device_id_type=MESH,
+        )
+
+    small = [
+        (owner_in, owner),
+        (lengths_in, lengths),
+        (hidden_in, hidden),
+        (attn_gain_in, attn_gain),
+        (freqs_in, freqs),
+        (ffn_gain_in, ffn_gain),
+    ]
+    small = [pltpu.make_async_copy(s, d, ssem.at[i]) for i, (s, d) in enumerate(small)]
+    for c in small:
+        c.start()
     loads = [
         (w_query.at[0], wqkv.at[:, pl.ds(0, 1024)]),
         (w_key.at[0], wqkv.at[:, pl.ds(1024, 128)]),
@@ -108,19 +148,10 @@
         (w_down.at[0], wd),
     ]
     loads = [pltpu.make_async_copy(s, d, wsem.at[i]) for i, (s, d) in enumerate(loads)]
-    for c in loads[:3]:
+    for c in loads:
         c.start()
-
-    barrier = pltpu.get_barrier_semaphore()
-    for o in OFFSETS:
-        pl.semaphore_signal(barrier, inc=1, device_id={"mem": peer(o)}, device_id_type=MESH)
-    for k in RING:
-        pl.semaphore_signal(
-            barrier, inc=1, device_id={"tp": lax.rem(tp + k, 8)}, device_id_type=MESH
-        )
-    pl.semaphore_signal(barrier, inc=1, device_id={"section": 1 - sec}, device_id_type=MESH)
-    for c in loads[3:]:
-        c.start()
+    for c in small:
+        c.wait()
 
     row = lax.broadcasted_iota(jnp.int32, (ROWS, ROWS), 0)
     col = lax.broadcasted_iota(jnp.int32, (ROWS, ROWS), 1)
@@ -142,15 +173,40 @@
     lane = lax.broadcasted_iota(jnp.int32, (8, 128), 1)
     sine = jnp.where(lane < 64, -sine, sine)
 
+    across_x2 = pltpu.make_async_remote_copy(
+        src_ref=x2,
+        dst_ref=x2in,
+        send_sem=send.at[7],
+        recv_sem=recv.at[7],
+        device_id={"section": 1 - sec},
+        device_id_type=MESH,
+    )
+    across_out = pltpu.make_async_remote_copy(
+        src_ref=xin,
+        dst_ref=xout,
+        send_sem=send.at[8],
+        recv_sem=recv.at[8],
+        device_id={"section": 1 - sec},
+        device_id_type=MESH,
+    )
+
     @pl.when(sec == 0)
     def _():
-        xin[...] = _nn(to_slots, hidden_in[...]).astype(BF16)
-
-    pl.semaphore_wait(barrier, 23)
+        xin[...] = _nn(to_slots, hidden[...]).astype(BF16)
+
+    def summed(rb, at):
+        total = rb[at].astype(F32)
+        for k in range(1, 8):
+            total = total + rb[at + k].astype(F32)
+        return total
 
     @pl.when(sec == 1)
     def _():
-        pltpu.make_async_copy(xout, xin, recv.at[7]).wait()
+        pl.semaphore_wait(barrier, BARRIER)
+        pltpu.make_async_copy(x2, x2in, recv.at[7]).wait()
+        pltpu.make_async_copy(rb6.at[pl.ds(0, 8)], rb6.at[pl.ds(0, 8)], recv6.at[0]).wait()
+        xin[...] = (x2in[...].astype(F32) + summed(rb6, 0)).astype(BF16)
+        across_out.start()
 
     x = xin[...].astype(F32)
     scaled = (x * attn_gain[...].astype(F32)).astype(BF16)
@@ -162,6 +218,10 @@
         sb1[pl.ds(h, ROWS, stride=12), :] = part[:, h * 128 : (h + 1) * 128]
     sb1[pl.ds(10, ROWS, stride=12), :] = jnp.broadcast_to(squares, (ROWS, 128))
     sb1[pl.ds(11, ROWS, stride=12), :] = jnp.zeros((ROWS, 128), F32)
+
+    @pl.when(sec == 0)
+    def _():
+        pl.semaphore_wait(barrier, BARRIER)
 
     def rows_of(m):
         return pl.ds(pl.multiple_of(m * 24, 8), 24)
@@ -235,40 +295,27 @@
 
     from7 = pl.ds(1, 7)
 
-    def tp_sum(part, sb, rb, which):
-        sb[...] = part.astype(BF16)
-        for k in RING:
-            pltpu.make_async_remote_copy(
-                src_ref=sb,
-                dst_ref=rb.at[tp],
-                send_sem=send.at[which],
-                recv_sem=recv.at[which],
-                device_id={"tp": lax.rem(tp + k, 8)},
-                device_id_type=MESH,
-            ).start()
-        rb[tp] = sb[...]
-        pltpu.make_async_copy(rb.at[from7], rb.at[from7], recv.at[which]).wait()
-        total = rb[0].astype(F32)
-        for k in range(1, 8):
-            total = total + rb[k].astype(F32)
-        return total
-
-    x = (x + tp_sum(part, sb3, rb3, 2)).astype(BF16).astype(F32)
+    sb3[...] = part.astype(BF16)
+    for k in RING:
+        pltpu.make_async_remote_copy(
+            src_ref=sb3,
+            dst_ref=rb3.at[tp],
+            send_sem=send.at[2],
+            recv_sem=recv.at[2],
+            device_id={"tp": lax.rem(tp + k, 8)},
+            device_id_type=MESH,
+        ).start()
+    rb3[tp] = sb3[...]
+    pltpu.make_async_copy(rb3.at[from7], rb3.at[from7], recv.at[2]).wait()
+    x = (x + summed(rb3, 0)).astype(BF16)
+    x2[...] = x
+    x = x.astype(F32)
 
     squares = jnp.sum(x * x, axis=1, keepdims=True)
     packed = jnp.zeros((8, 128), F32)
     for g in range(4):
         packed = jnp.where(lane // 32 == g, squares[8 * g : 8 * g + 8], packed)
     ssq[...] = packed
-    for o in OFFSETS:
-        pltpu.make_async_remote_copy(
-            src_ref=ssq,
-            dst_ref=rsq.at[slot_at(o)],
-            send_sem=send.at[3],
-            recv_sem=recv.at[3],
-            device_id={"mem": peer(o)},
-            device_id_type=MESH,
-        ).start()
     scaled = (x * ffn_gain[...].astype(F32)).astype(BF16)
     loads[8].wait()
     loads[9].wait()
@@ -281,8 +328,18 @@
         both = jnp.concatenate([wg[:, columns(j)], wu[:, columns(j)]], axis=1)
         return _nn(scaled, both)
 
-    groups = (OFFSETS[:5], OFFSETS[5:11], OFFSETS[11:])
-    for group in groups:
+    far_first = (OFFSETS[:5], OFFSETS[5:11], OFFSETS[11:])
+    near_first = far_first[::-1]
+    for group in far_first:
+        for o in group:
+            pltpu.make_async_remote_copy(
+                src_ref=ssq,
+                dst_ref=rsq.at[slot_at(o)],
+                send_sem=send.at[3],
+                recv_sem=recv.at[3],
+                device_id={"mem": peer(o)},
+                device_id_type=MESH,
+            ).start()
         for o in group:
             sb4[o[0] * 4 + o[1]] = units(peer(o)).astype(BF16)
         for o in group:
@@ -293,10 +350,14 @@
                     src_ref=sb4.at[o[0] * 4 + o[1]],
                     dst_ref=rb4.at[slot_at(o)],
                     send_sem=send.at[4],
-                    recv_sem=recv.at[4],
+                    recv_sem=recv4.at[slot_at(o)],
                     device_id={"mem": peer(o)},
                     device_id_type=MESH,
                 ).start()
+
+    @pl.when(sec == 0)
+    def _():
+        across_x2.start()
 
     sums = units(mem)
     pltpu.make_async_copy(rsq.at[from15], rsq.at[from15], recv.at[3]).wait()
@@ -307,10 +368,12 @@
 
     @pl.when(mem < OWNERS)
     def _():
-        pltpu.make_async_copy(rb4.at[from15], rb4.at[from15], recv.at[4]).wait()
         own_units = sums
-        for k in range(1, 16):
-            own_units = own_units + rb4[k].astype(F32)
+        for group in near_first:
+            for k in [o[0] * 4 + o[1] for o in group]:
+                pltpu.make_async_copy(rb4.at[k], rb4.at[k], recv4.at[k]).wait()
+            for k in [o[0] * 4 + o[1] for o in group]:
+                own_units = own_units + rb4[k].astype(F32)
         own_units = own_units * factor
         gate, up = own_units[:, :128], own_units[:, 128:]
         units_here = (gate / (1.0 + jnp.exp(-gate)) * up).astype(BF16)
@@ -321,44 +384,72 @@
                 src_ref=sb5,
                 dst_ref=rb5.at[mem],
                 send_sem=send.at[5],
-                recv_sem=recv.at[5],
+                recv_sem=recv5.at[slot_at(o)],
                 device_id={"mem": peer(o)},
                 device_id_type=MESH,
             ).start()
-        from13 = pl.ds(0, 13)
-        pltpu.make_async_copy(rb5.at[from13], rb5.at[from13], recv.at[5]).wait()
 
     @pl.when(mem >= OWNERS)
     def _():
-        from14 = pl.ds(0, 14)
-        pltpu.make_async_copy(rb5.at[from14], rb5.at[from14], recv.at[5]).wait()
+        rb5[mem] = jnp.zeros((ROWS, 128), BF16)
 
     loads[10].wait()
-    hidden = jnp.concatenate([rb5[j] for j in range(OWNERS)], axis=1)
-    part = _nn(hidden, wd[...])
-    x = (x + tp_sum(part, sb6, rb6, 6)).astype(BF16)
-    xout[...] = x
-
-    across = pltpu.make_async_remote_copy(
-        src_ref=xout,
-        dst_ref=xin,
-        send_sem=send.at[7],
-        recv_sem=recv.at[7],
+    part = jnp.zeros((ROWS, 512), F32)
+    for group in ([(0, 0)] + near_first[0],) + near_first[1:]:
+        for o in group:
+            if o != (0, 0):
+
+                @pl.when(peer(o) < OWNERS)
+                def _(o=o):
+                    k = o[0] * 4 + o[1]
+                    pltpu.make_async_copy(rb5.at[k], rb5.at[k], recv5.at[k]).wait()
+
+                @pl.when(peer(o) >= OWNERS)
+                def _(o=o):
+                    rb5[peer(o)] = jnp.zeros((ROWS, 128), BF16)
+
+        theirs = jnp.concatenate([rb5[peer(o)] for o in group], axis=1)
+        down = jnp.concatenate(
+            [wd[columns(jnp.minimum(peer(o), OWNERS - 1)), :] for o in group], axis=0
+        )
+        part = part + _nn(theirs, down)
+    sb6[...] = part.astype(BF16)
+    for k in RING:
+        pltpu.make_async_remote_copy(
+            src_ref=sb6,
+            dst_ref=rb6.at[sec * 8 + tp],
+            send_sem=send.at[6],
+            recv_sem=recv6.at[sec],
+            device_id={"section": 1, "tp": lax.rem(tp + k, 8)},
+            device_id_type=MESH,
+        ).start()
+    across_own = pltpu.make_async_remote_copy(
+        src_ref=sb6,
+        dst_ref=rb6.at[tp],
+        send_sem=send.at[6],
+        recv_sem=recv6.at[0],
         device_id={"section": 1 - sec},
         device_id_type=MESH,
     )
 
     @pl.when(sec == 0)
     def _():
-        across.start()
-
-    out[0] = _nn(to_requests, x).astype(BF16)
+        across_own.start()
+        pltpu.make_async_copy(xin, xout, recv.at[8]).wait()
+
+    @pl.when(sec == 1)
+    def _():
+        rb6[8 + tp] = sb6[...]
+        from8 = pl.ds(8, 7)
+        pltpu.make_async_copy(rb6.at[from8], rb6.at[from8], recv6.at[1]).wait()
+        xout[...] = (x2[...].astype(F32) + summed(rb6, 8)).astype(BF16)
+
+    out[0] = _nn(to_requests, xout[...]).astype(BF16)
 
     pltpu.make_async_copy(rb1.at[from15], rb1.at[from15], send.at[0]).wait()
     pltpu.make_async_copy(rb2.at[from15], rb2.at[from15], send.at[1]).wait()
     pltpu.make_async_copy(rb3.at[from7], rb3.at[from7], send.at[2]).wait()
     pltpu.make_async_copy(rsq.at[from15], rsq.at[from15], send.at[3]).wait()
-    pltpu.make_async_copy(rb6.at[from7], rb6.at[from7], send.at[6]).wait()
 
     @pl.when(mem < OWNERS)
     def _():
@@ -374,7 +465,14 @@
 
     @pl.when(sec == 0)
     def _():
-        across.wait_send()
+        all8 = pl.ds(0, 8)
+        pltpu.make_async_copy(rb6.at[all8], rb6.at[all8], send.at[6]).wait()
+        across_x2.wait_send()
+
+    @pl.when(sec == 1)
+    def _():
+        pltpu.make_async_copy(rb6.at[from7], rb6.at[from7], send.at[6]).wait()
+        across_out.wait_send()
 
 
 FREQS = (500000.0 ** (-(np.arange(64, dtype=np.float64) * 2.0) / 128)).astype(np.float32)
@@ -383,16 +481,21 @@
 
 def per_device(hidden_in, lengths, owner_order, attn_gain, w_query, w_key, w_value, w_out,
                ffn_gain, w_gate, w_up, w_down, key_cache, value_cache):
-    smem = pl.BlockSpec(memory_space=pltpu.SMEM)
     vmem = pl.BlockSpec(memory_space=pltpu.VMEM)
     hbm = pl.BlockSpec(memory_space=pl.ANY)
     V = pltpu.VMEM
     return pl.pallas_call(
         kernel,
-        out_shape=jax.ShapeDtypeStruct((1, ROWS, 512), BF16),
-        in_specs=[smem, smem, vmem, vmem, vmem, vmem] + [hbm] * 9,
+        out_shape=pltpu.VMEM((1, ROWS, 512), BF16),
+        in_specs=[hbm] * 15,
         out_specs=vmem,
         scratch_shapes=[
+            pltpu.SMEM((ROWS,), jnp.int32),
+            pltpu.SMEM((ROWS,), jnp.int32),
+            V((1, 128), F32),
+            V((ROWS, 512), BF16),
+            V((1, 512), BF16),
+            V((1, 512), BF16),
             V((512, 1280), BF16),
             V((1024, 512), BF16),
             V((512, 1792), BF16),
@@ -402,6 +505,8 @@
             V((CTX, 256), BF16),
             V((ROWS, 512), BF16),
             V((ROWS, 512), BF16),
+            V((ROWS, 512), BF16),
+            V((ROWS, 512), BF16),
             V((384, 128), F32),
             V((16, 24, 128), F32),
             V((16, 128), BF16),
@@ -416,10 +521,14 @@
             V((ROWS, 128), BF16),
             V((16, ROWS, 128), BF16),
             V((ROWS, 512), BF16),
-            V((8, ROWS, 512), BF16),
+            V((16, ROWS, 512), BF16),
+            pltpu.SemaphoreType.DMA((6,)),
             pltpu.SemaphoreType.DMA((11,)),
-            pltpu.SemaphoreType.DMA((8,)),
-            pltpu.SemaphoreType.DMA((8,)),
+            pltpu.SemaphoreType.DMA((9,)),
+            pltpu.SemaphoreType.DMA((9,)),
+            pltpu.SemaphoreType.DMA((16,)),
+            pltpu.SemaphoreType.DMA((16,)),
+            pltpu.SemaphoreType.DMA((2,)),
         ],
         compiler_params=pltpu.CompilerParams(
             collective_id=0, has_side_effects=True, vmem_limit_bytes=56 << 20

time: 79.5 us -> 76.7 us (0.965)
  Pallas kernels: 77.9 us -> 76 us
    pallas_call x1, Pallas kernels: 77.9 us -> 76 us  [per_device(): pl.pallas_call(kernel, out_shape=pltpu.VMEM((1, ROWS, 512), BF16), in_spe...]
where the time goes in v2:
time: 76.7 us; the launch traced here: 76.6 us
  Pallas kernels  76 us (99%)
    pallas_call x1, Pallas kernels, per_device(): pl.pallas_call(kernel, out_shape=pltpu.VMEM((1, ROWS, 512), BF16), in_spe...  76 us

profile of v2, /device:TPU:1, one launch (start us, length us, event | category | flops | bytes accessed | tf_op | source)
XLA Modules:
  0.0 76.6 jit_solution(13955800831731112632)
XLA Ops:
  0.0 76.0 %shard_map.145 = bf16[1,32,512]{2,1,0:T(8,128)(2,1)S(1)} custom-call(s32[32]{0:T(128)} %lengths_in.1, s32[32]{0:T(128)} %owner_in.1, f32[1,128]{1,0:T(1,128)} %constant.2.clone.freqs_in, bf16[32,512]{1,0:T(8,128)(2,1)} %hidden_in.1, bf16[1,512]{1,0:T(2,128)(2,1)} %attn_gain_in.1, bf16[1,512]{1,0:T(2,128)(2,1)} %ffn_gain_in.1, bf16[1,512,1024]{2,1,0:T(8,128)(2,1)} %w_query.1, ...), custom_call_target="tpu_custom_call" | custom-call | tf_op jit(solution)/shard_map/pallas_call | solution.py:487
  76.0 0.6 copy.17

commit v3 on v1

v3 whole, which is shorter than its diff:
```python
import functools
import math

import jax
import jax.numpy as jnp
import numpy as np
from jax import lax
from jax.experimental import pallas as pl
from jax.experimental.pallas import tpu as pltpu
from jax.sharding import PartitionSpec as P

D = 8192
HD = 128
CTX = 4096
ROWS = 32
EPS = 1e-05
MESH = pl.DeviceIdType.MESH
F32 = jnp.float32
BF16 = jnp.bfloat16


def _hops(o):
    return min(o[0], 4 - o[0]) + min(o[1], 4 - o[1])


OFFSETS = sorted(
    [(a, b) for a in range(4) for b in range(4) if (a, b) != (0, 0)], key=lambda o: -_hops(o)
)
RING = (4, 3, 5, 2, 6, 1, 7)
OWNERS = 14


def _nt(a, b):
    return lax.dot_general(a, b, (((1,), (1,)), ((), ())), preferred_element_type=F32)


def _nn(a, b):
    return jnp.dot(a, b, preferred_element_type=F32)


def kernel(
    lengths_in,
    owner_in,
    freqs_in,
    hidden_in,
    attn_gain_in,
    ffn_gain_in,
    w_query,
    w_key,
    w_value,
    w_out,
    w_gate,
    w_up,
    w_down,
    key_cache,
    value_cache,
    out,
    lengths,
    owner,
    freqs,
    hidden,
    attn_gain,
    ffn_gain,
    wqkv,
    kbuf,
    vbuf,
    wo,
    wg,
    wu,
    wd,
    states,
    xout,
    sb1,
    rb1,
    sb2,
    rb2,
    fb2,
    sb3,
    rb3,
    ssq,
    rsq,
    sb4,
    rb4,
    sb5,
    rb5,
    sb6,
    rb6,
    ssem,
    wsem,
    push_send,
    push_recv,
    send1,
    recv1,
    send2,
    recv2,
    send3,
    recv3,
    sendq,
    recvq,
    send4,
    recv4,
    send5,
    recv5,
    send6,
    recv6,
    sendx,
    recvx,
):
    sec = lax.axis_index("section")
    tp = lax.axis_index("tp")
    mem = lax.axis_index("mem")
    my, mx = mem // 4, lax.rem(mem, 4)

    def peer(o):
        return lax.rem(my + o[0], 4) * 4 + lax.rem(mx + o[1], 4)

    def slot_at(o):
        return ((4 - o[0]) % 4) * 4 + (4 - o[1]) % 4

    def remote(src, dst, sent, arrived, **device):
        return pltpu.make_async_remote_copy(
            src_ref=src,
            dst_ref=dst,
            send_sem=sent,
            recv_sem=arrived,
            device_id=device,
            device_id_type=MESH,
        )

    def wait_for(ref, sem):
        pltpu.make_async_copy(ref, ref, sem).wait()

    barrier = pltpu.get_barrier_semaphore()

    def greet(**device):
        pl.semaphore_signal(barrier, inc=1, device_id=device, device_id_type=MESH)

    @pl.when(sec == 0)
    def _():
        for o in OFFSETS:
            greet(mem=peer(o))
        greet(section=1)

    @pl.when(sec == 1)
    def _():
        for o in OFFSETS:
            greet(section=0, mem=peer(o))
        greet(section=0)
        for o in OFFSETS:
            greet(mem=peer(o))
        for k in RING:
            greet(tp=lax.rem(tp + k, 8))

    small = [
        (owner_in, owner),
        (lengths_in, lengths),
        (hidden_in, hidden),
        (attn_gain_in, attn_gain),
        (freqs_in, freqs),
    ]
    small = [pltpu.make_async_copy(s, d, ssem.at[i]) for i, (s, d) in enumerate(small)]
    loads = [
        (w_query.at[0], wqkv.at[:, pl.ds(0, 1024)]),
        (w_key.at[0], wqkv.at[:, pl.ds(1024, 128)]),
        (w_value.at[0], wqkv.at[:, pl.ds(1152, 128)]),
        (key_cache.at[0, 0], kbuf.at[:, pl.ds(0, 128)]),
        (key_cache.at[0, 1], kbuf.at[:, pl.ds(128, 128)]),
        (value_cache.at[0, 0], vbuf.at[:, pl.ds(0, 128)]),
        (value_cache.at[0, 1], vbuf.at[:, pl.ds(128, 128)]),
    ]
    later = [
        (w_out.at[0], wo),
        (ffn_gain_in, ffn_gain),
        (w_gate.at[0], wg),
        (w_up.at[0], wu),
        (w_down.at[0], wd),
    ]
    pushes = [
        remote(s, d.at[0], push_send.at[i], push_recv.at[i], section=1 - sec)
        for i, (s, d) in enumerate(later)
    ]
    later = [
        pltpu.make_async_copy(s, d.at[1], wsem.at[7 + i]) for i, (s, d) in enumerate(later)
    ]
    loads = [pltpu.make_async_copy(s, d, wsem.at[i]) for i, (s, d) in enumerate(loads)]
    for c in small + loads[:3]:
        c.start()
    for c in small:
        c.wait()

    row = lax.broadcasted_iota(jnp.int32, (ROWS, ROWS), 0)
    col = lax.broadcasted_iota(jnp.int32, (ROWS, ROWS), 1)
    by_row = jnp.zeros((ROWS, ROWS), jnp.int32)
    by_col = jnp.zeros((ROWS, ROWS), jnp.int32)
    for j in range(ROWS):
        r = owner[j]
        by_row = jnp.where(row == j, r, by_row)
        by_col = jnp.where(col == j, r, by_col)
    to_slots = jnp.where(by_row == col, 1.0, 0.0).astype(BF16)
    to_requests = jnp.where(by_col == row, 1.0, 0.0).astype(BF16)
    states[0] = _nn(to_slots, hidden[...]).astype(BF16)

    len0 = lengths[owner[2 * mem]]
    len1 = lengths[owner[2 * mem + 1]]
    upper = lax.broadcasted_iota(jnp.int32, (8, 128), 0) < 4
    angles = jnp.where(upper, len0, len1).astype(F32) * freqs[...]
    cosine = jnp.cos(angles)
    sine = jnp.sin(angles)
    lane = lax.broadcasted_iota(jnp.int32, (8, 128), 1)
    sine = jnp.where(lane < 64, -sine, sine)

    from15 = pl.ds(1, 15)
    from7 = pl.ds(1, 7)
    far_first = (OFFSETS[:5], OFFSETS[5:11], OFFSETS[11:])
    near_first = far_first[::-1]

    def index(o):
        return o[0] * 4 + o[1]

    def columns(j):
        return pl.ds(pl.multiple_of(j * 128, 128), 128)

    handover = remote(states.at[1], xout, sendx, recvx, section=1 - sec)

    def rest_of(layer):
        mine = rb2.at[layer]
        if layer == 0:
            wait_for(mine, recv2.at[0])
        else:
            wait_for(mine.at[from15], recv2.at[1])

        def ready(i):
            if layer == 0:
                pushes[i].wait_recv()
            else:
                later[i].wait()

        ready(0)
        fb2[...] = mine[...].astype(F32).reshape(256, 128)
        wide = jnp.concatenate([fb2[pl.ds(h, ROWS, stride=8), :] for h in range(8)], axis=1)
        part = _nn(wide.astype(BF16), wo[layer])

        def tp_sum(part, sb, rb, sent, arrived):
            sb[layer] = part.astype(BF16)
            for k in RING:
                remote(
                    sb.at[layer],
                    rb.at[layer, tp],
                    sent.at[layer],
                    arrived.at[layer],
                    tp=lax.rem(tp + k, 8),
                ).start()
            rb[layer, tp] = sb[layer]
            wait_for(rb.at[layer, from7], arrived.at[layer])
            total = rb[layer, 0].astype(F32)
            for k in range(1, 8):
                total = total + rb[layer, k].astype(F32)
            return total

        x = states[layer].astype(F32) + tp_sum(part, sb3, rb3, send3, recv3)
        x = x.astype(BF16).astype(F32)

        squares = jnp.sum(x * x, axis=1, keepdims=True)
        packed = jnp.zeros((8, 128), F32)
        for g in range(4):
            packed = jnp.where(lane // 32 == g, squares[8 * g : 8 * g + 8], packed)
        ssq[layer] = packed
        ready(1)
        scaled = (x * ffn_gain[layer].astype(F32)).astype(BF16)
        ready(2)
        ready(3)

        def units(j):
            j = jnp.minimum(j, OWNERS - 1)
            both = jnp.concatenate([wg[layer, :, columns(j)], wu[layer, :, columns(j)]], axis=1)
            return _nn(scaled, both)

        for group in far_first:
            for o in group:
                remote(
                    ssq.at[layer],
                    rsq.at[layer, slot_at(o)],
                    sendq.at[layer],
                    recvq.at[layer],
                    mem=peer(o),
                ).start()
            for o in group:
                sb4[layer, index(o)] = units(peer(o)).astype(BF16)
            for o in group:

                @pl.when(peer(o) < OWNERS)
                def _(o=o):
                    remote(
                        sb4.at[layer, index(o)],
                        rb4.at[layer, slot_at(o)],
                        send4.at[layer],
                        recv4.at[layer, slot_at(o)],
                        mem=peer(o),
                    ).start()

        sums = units(mem)
        wait_for(rsq.at[layer, from15], recvq.at[layer])
        for k in range(1, 16):
            packed = packed + rsq[layer, k]
        packed = lax.rsqrt(packed / D + EPS)
        factor = jnp.concatenate([packed[:, 32 * g : 32 * g + 1] for g in range(4)], axis=0)

        @pl.when(mem < OWNERS)
        def _():
            own_units = sums
            for group in near_first:
                for k in [index(o) for o in group]:
                    wait_for(rb4.at[layer, k], recv4.at[layer, k])
                for k in [index(o) for o in group]:
                    own_units = own_units + rb4[layer, k].astype(F32)
            own_units = own_units * factor
            gate, up = own_units[:, :128], own_units[:, 128:]
            here = (gate / (1.0 + jnp.exp(-gate)) * up).astype(BF16)
            sb5[layer] = here
            rb5[layer, mem] = here
            for o in OFFSETS:
                remote(
                    sb5.at[layer],
                    rb5.at[layer, mem],
                    send5.at[layer],
                    recv5.at[layer, slot_at(o)],
                    mem=peer(o),
                ).start()

        @pl.when(mem >= OWNERS)
        def _():
            rb5[layer, mem] = jnp.zeros((ROWS, 128), BF16)

        ready(4)
        part = jnp.zeros((ROWS, 512), F32)
        for group in ([(0, 0)] + near_first[0],) + near_first[1:]:
            for o in group:
                if o != (0, 0):

                    @pl.when(peer(o) < OWNERS)
                    def _(o=o):
                        k = index(o)
                        wait_for(rb5.at[layer, k], recv5.at[layer, k])

                    @pl.when(peer(o) >= OWNERS)
                    def _(o=o):
                        rb5[layer, peer(o)] = jnp.zeros((ROWS, 128), BF16)

            theirs = jnp.concatenate([rb5[layer, peer(o)] for o in group], axis=1)
            down = jnp.concatenate(
                [wd[layer, columns(jnp.minimum(peer(o), OWNERS - 1)), :] for o in group], axis=0
            )
            part = part + _nn(theirs, down)
        return (x + tp_sum(part, sb6, rb6, send6, recv6)).astype(BF16)

    @pl.when(sec == 1)
    def _():
        for c in loads[3:] + later:
            c.start()
        pl.semaphore_wait(barrier, 23)
        states[1] = rest_of(0)
        handover.start()

    x = states[sec].astype(F32)
    scaled = (x * attn_gain[...].astype(F32)).astype(BF16)
    squares = jnp.sum(x * x, axis=1, keepdims=True)
    for c in loads[:3]:
        c.wait()

    @pl.when(sec == 0)
    def _():
        for c in loads[3:]:
            c.start()

    part = _nn(scaled, wqkv[...])
    for h in range(10):
        sb1[pl.ds(h, ROWS, stride=12), :] = part[:, h * 128 : (h + 1) * 128]
    sb1[pl.ds(10, ROWS, stride=12), :] = jnp.broadcast_to(squares, (ROWS, 128))
    sb1[pl.ds(11, ROWS, stride=12), :] = jnp.zeros((ROWS, 128), F32)

    @pl.when(sec == 0)
    def _():
        pl.semaphore_wait(barrier, 31)

    def rows_of(m):
        return pl.ds(pl.multiple_of(m * 24, 8), 24)

    for o in OFFSETS:
        remote(
            sb1.at[rows_of(peer(o))], rb1.at[slot_at(o)], send1, recv1, mem=peer(o)
        ).start()

    @pl.when(sec == 0)
    def _():
        for c in pushes[:3]:
            c.start()

    heads = sb1[rows_of(mem), :]
    wait_for(rb1.at[from15], recv1)
    for k in range(1, 16):
        heads = heads + rb1[k]

    def turned(v, s):
        c, n = cosine[4 * s : 4 * s + 1], sine[4 * s : 4 * s + 1]
        return v * c + pltpu.roll(v, 64, 1) * n

    scale = 1.0 / math.sqrt(HD)
    zero = jnp.zeros((8, 128), F32)
    queries, owns, values = [], [], []
    for s in range(2):
        mine = heads[12 * s : 12 * s + 12]
        mine = mine * lax.rsqrt(mine[10:11] / D + EPS)
        q = turned(mine[0:8], s)
        kv = turned(mine[8:9], s).astype(BF16).astype(F32)
        values.append(jnp.broadcast_to(mine[9:10].astype(BF16).astype(F32), (8, 128)))
        q = q.astype(BF16).astype(F32)
        owns.append(jnp.sum(q * kv, axis=1, keepdims=True) * scale)
        queries.append(jnp.concatenate([q, zero] if s == 0 else [zero, q], axis=1))
    queries = jnp.concatenate(queries, axis=0).astype(BF16)
    own_score = jnp.concatenate(owns, axis=0)
    new_values = jnp.concatenate(values, axis=0)
    loads[3].wait()
    loads[4].wait()
    scores = _nt(queries, kbuf[...]) * scale
    where = lax.broadcasted_iota(jnp.int32, (16, CTX), 1)
    first = lax.broadcasted_iota(jnp.int32, (16, 1), 0) < 8
    scores = jnp.where(where < jnp.where(first, len0, len1), scores, -jnp.inf)
    peak = jnp.maximum(jnp.max(scores, axis=1, keepdims=True), own_score)
    soft = jnp.exp(scores - peak)
    own = jnp.exp(own_score - peak)
    total = jnp.sum(soft, axis=1, keepdims=True) + own
    loads[5].wait()
    loads[6].wait()
    mixed = _nn(soft.astype(BF16), vbuf[...])
    mixed = jnp.where(first, mixed[:, :128], mixed[:, 128:])
    mixed = mixed + own.astype(BF16).astype(F32) * new_values
    attended = (mixed / total).astype(BF16)
    sb2[...] = attended
    for o in OFFSETS:
        remote(sb2, rb2.at[sec, mem], send2, recv2.at[sec], section=1, mem=peer(o)).start()

    across = remote(sb2, rb2.at[0, mem], send2, recv2.at[0], section=1 - sec)

    @pl.when(sec == 0)
    def _():
        across.start()
        for c in pushes[3:]:
            c.start()
        handover.wait_recv()

    @pl.when(sec == 1)
    def _():
        rb2[1, mem] = attended
        xout[...] = rest_of(1)

    out[0] = _nn(to_requests, xout[...]).astype(BF16)

    wait_for(rb1.at[from15], send1)

    @pl.when(sec == 0)
    def _():
        wait_for(rb2.at[0], send2)
        for c in pushes:
            c.wait_send()

    @pl.when(sec == 1)
    def _():
        wait_for(rb2.at[0, from15], send2)
        handover.wait_send()
        for layer in range(2):
            wait_for(rb3.at[layer, from7], send3.at[layer])
            wait_for(rsq.at[layer, from15], sendq.at[layer])
            wait_for(rb6.at[layer, from7], send6.at[layer])

            @pl.when(mem < OWNERS)
            def _(layer=layer):
                wait_for(rb4.at[layer, pl.ds(0, 13)], send4.at[layer])
                wait_for(rb5.at[layer, pl.ds(0, 15)], send5.at[layer])

            @pl.when(mem >= OWNERS)
            def _(layer=layer):
                wait_for(rb4.at[layer, pl.ds(0, 14)], send4.at[layer])


FREQS = (500000.0 ** (-(np.arange(64, dtype=np.float64) * 2.0) / 128)).astype(np.float32)
FREQS = np.concatenate([FREQS, FREQS])[None, :]


def per_device(hidden_in, lengths, owner_order, attn_gain, w_query, w_key, w_value, w_out,
               ffn_gain, w_gate, w_up, w_down, key_cache, value_cache):
    vmem = pl.BlockSpec(memory_space=pltpu.VMEM)
    hbm = pl.BlockSpec(memory_space=pl.ANY)
    V, S = pltpu.VMEM, pltpu.SemaphoreType.DMA
    return pl.pallas_call(
        kernel,
        out_shape=pltpu.VMEM((1, ROWS, 512), BF16),
        in_specs=[hbm] * 15,
        out_specs=vmem,
        scratch_shapes=[
            pltpu.SMEM((ROWS,), jnp.int32),
            pltpu.SMEM((ROWS,), jnp.int32),
            V((1, 128), F32),
            V((ROWS, 512), BF16),
            V((1, 512), BF16),
            V((2, 1, 512), BF16),
            V((512, 1280), BF16),
            V((CTX, 256), BF16),
            V((CTX, 256), BF16),
            V((2, 1024, 512), BF16),
            V((2, 512, 1792), BF16),
            V((2, 512, 1792), BF16),
            V((2, 1792, 512), BF16),
            V((2, ROWS, 512), BF16),
            V((ROWS, 512), BF16),
            V((384, 128), F32),
            V((16, 24, 128), F32),
            V((16, 128), BF16),
            V((2, 16, 16, 128), BF16),
            V((256, 128), F32),
            V((2, ROWS, 512), BF16),
            V((2, 8, ROWS, 512), BF16),
            V((2, 8, 128), F32),
            V((2, 16, 8, 128), F32),
            V((2, 16, ROWS, 256), BF16),
            V((2, 16, ROWS, 256), BF16),
            V((2, ROWS, 128), BF16),
            V((2, 16, ROWS, 128), BF16),
            V((2, ROWS, 512), BF16),
            V((2, 8, ROWS, 512), BF16),
            S((5,)),
            S((12,)),
            S((5,)),
            S((5,)),
            S(()),
            S(()),
            S(()),
            S((2,)),
            S((2,)),
            S((2,)),
            S((2,)),
            S((2,)),
            S((2,)),
            S((2, 16)),
            S((2,)),
            S((2, 16)),
            S((2,)),
            S((2,)),
            S(()),
            S(()),
        ],
        compiler_params=pltpu.CompilerParams(
            collective_id=0, has_side_effects=True, vmem_limit_bytes=56 << 20
        ),
    )(
        lengths, owner_order, jnp.asarray(FREQS), hidden_in, attn_gain, ffn_gain,
        w_query, w_key, w_value, w_out, w_gate, w_up, w_down, key_cache, value_cache,
    )


def solution(mesh):
    placed = (
        P(None, "mem"),
        P(),
        P(),
        P("section", "mem"),
        P("section", "mem", "tp"),
        P("section", "mem", "tp"),
        P("section", "mem", "tp"),
        P("section", "tp", "mem"),
        P("section", "mem"),
        P("section", "mem", "tp"),
        P("section", "mem", "tp"),
        P("section", "tp", "mem"),
        P("section", "mem", None, "tp"),
        P("section", "mem", None, "tp"),
    )
    return jax.shard_map(
        per_device, mesh=mesh, in_specs=placed, out_specs=P("section", None, "mem"), check_vma=False
    )
```

time: 79.5 us -> 72.3 us (0.909)
  Pallas kernels: 77.9 us -> 71.6 us
    pallas_call x1, Pallas kernels: 77.9 us -> 71.6 us  [per_device(): pl.pallas_call(kernel, out_shape=pltpu.VMEM((1, ROWS, 512), BF16), in_spe...]
where the time goes in v3:
time: 72.3 us; the launch traced here: 72.2 us
  Pallas kernels  71.6 us (99%)
    pallas_call x1, Pallas kernels, per_device(): pl.pallas_call(kernel, out_shape=pltpu.VMEM((1, ROWS, 512), BF16), in_spe...  71.6 us

profile of v3, /device:TPU:1, one launch (start us, length us, event | category | flops | bytes accessed | tf_op | source)
XLA Modules:
  0.0 72.2 jit_solution(6439033872332623120)
XLA Ops:
  0.0 71.6 %shard_map.145 = bf16[1,32,512]{2,1,0:T(8,128)(2,1)S(1)} custom-call(s32[32]{0:T(128)} %lengths_in.1, s32[32]{0:T(128)} %owner_in.1, f32[1,128]{1,0:T(1,128)} %constant.2.clone.freqs_in, bf16[32,512]{1,0:T(8,128)(2,1)} %hidden_in.1, bf16[1,512]{1,0:T(2,128)(2,1)} %attn_gain_in.1, bf16[1,512]{1,0:T(2,128)(2,1)} %ffn_gain_in.1, bf16[1,512,1024]{2,1,0:T(8,128)(2,1)} %w_query.1, ...), custom_call_target="tpu_custom_call" | custom-call | tf_op jit(solution)/shard_map/pallas_call | solution.py:494
  71.6 0.6 copy.17

commit v4 on v3

v4 whole, which is shorter than its diff:
```python
import functools
import math

import jax
import jax.numpy as jnp
import numpy as np
from jax import lax
from jax.experimental import pallas as pl
from jax.experimental.pallas import tpu as pltpu
from jax.sharding import PartitionSpec as P

D = 8192
HD = 128
CTX = 4096
ROWS = 32
EPS = 1e-05
MESH = pl.DeviceIdType.MESH
F32 = jnp.float32
BF16 = jnp.bfloat16


def _hops(o):
    return min(o[0], 4 - o[0]) + min(o[1], 4 - o[1])


OFFSETS = sorted(
    [(a, b) for a in range(4) for b in range(4) if (a, b) != (0, 0)], key=lambda o: -_hops(o)
)
RING = (4, 3, 5, 2, 6, 1, 7)
OWNERS = 14


def _nt(a, b):
    return lax.dot_general(a, b, (((1,), (1,)), ((), ())), preferred_element_type=F32)


def _nn(a, b):
    return jnp.dot(a, b, preferred_element_type=F32)


def kernel(
    lengths_in,
    owner_in,
    freqs_in,
    hidden_in,
    attn_gain_in,
    ffn_gain_in,
    w_query,
    w_key,
    w_value,
    w_out,
    w_gate,
    w_up,
    w_down,
    key_cache,
    value_cache,
    out,
    lengths,
    owner,
    freqs,
    hidden,
    attn_gain,
    ffn_gain,
    wqkv,
    kbuf,
    vbuf,
    wo,
    wg,
    wu,
    wd,
    states,
    xout,
    sw1,
    sb1,
    rb1,
    sb2,
    rb2,
    fb2,
    sb3,
    rb3,
    ssq,
    rsq,
    sb4,
    rb4,
    sb5,
    rb5,
    sb6,
    rb6,
    ssem,
    wsem,
    push_send,
    push_recv,
    send1,
    recv1,
    send2,
    recv2,
    send3,
    recv3,
    sendq,
    recvq,
    send4,
    recv4,
    send5,
    recv5,
    send6,
    recv6,
    sendx,
    recvx,
):
    sec = lax.axis_index("section")
    tp = lax.axis_index("tp")
    mem = lax.axis_index("mem")
    my, mx = mem // 4, lax.rem(mem, 4)

    def peer(o):
        return lax.rem(my + o[0], 4) * 4 + lax.rem(mx + o[1], 4)

    def slot_at(o):
        return ((4 - o[0]) % 4) * 4 + (4 - o[1]) % 4

    def remote(src, dst, sent, arrived, **device):
        return pltpu.make_async_remote_copy(
            src_ref=src,
            dst_ref=dst,
            send_sem=sent,
            recv_sem=arrived,
            device_id=device,
            device_id_type=MESH,
        )

    def wait_for(ref, sem):
        pltpu.make_async_copy(ref, ref, sem).wait()

    barrier = pltpu.get_barrier_semaphore()

    def greet(**device):
        pl.semaphore_signal(barrier, inc=1, device_id=device, device_id_type=MESH)

    @pl.when(sec == 0)
    def _():
        for o in OFFSETS:
            greet(mem=peer(o))
        greet(section=1)

    @pl.when(sec == 1)
    def _():
        for o in OFFSETS:
            greet(section=0, mem=peer(o))
        greet(section=0)
        for o in OFFSETS:
            greet(mem=peer(o))
        for k in RING:
            greet(tp=lax.rem(tp + k, 8))

    small = [
        (owner_in, owner),
        (lengths_in, lengths),
        (hidden_in, hidden),
        (attn_gain_in, attn_gain),
        (freqs_in, freqs),
    ]
    small = [pltpu.make_async_copy(s, d, ssem.at[i]) for i, (s, d) in enumerate(small)]
    loads = [
        (w_query.at[0], wqkv.at[:, pl.ds(0, 1024)]),
        (w_key.at[0], wqkv.at[:, pl.ds(1024, 128)]),
        (w_value.at[0], wqkv.at[:, pl.ds(1152, 128)]),
        (key_cache.at[0, 0], kbuf.at[0]),
        (value_cache.at[0, 0], vbuf.at[0]),
        (key_cache.at[0, 1], kbuf.at[1]),
        (value_cache.at[0, 1], vbuf.at[1]),
    ]
    later = [
        (w_out.at[0], wo),
        (ffn_gain_in, ffn_gain),
        (w_gate.at[0], wg),
        (w_up.at[0], wu),
        (w_down.at[0], wd),
    ]
    pushes = [
        remote(s, d.at[0], push_send.at[i], push_recv.at[i], section=1 - sec)
        for i, (s, d) in enumerate(later)
    ]
    later = [
        pltpu.make_async_copy(s, d.at[1], wsem.at[7 + i]) for i, (s, d) in enumerate(later)
    ]
    loads = [pltpu.make_async_copy(s, d, wsem.at[i]) for i, (s, d) in enumerate(loads)]
    for c in small + loads[:3]:
        c.start()
    for c in small:
        c.wait()

    row = lax.broadcasted_iota(jnp.int32, (ROWS, ROWS), 0)
    col = lax.broadcasted_iota(jnp.int32, (ROWS, ROWS), 1)
    by_row = jnp.zeros((ROWS, ROWS), jnp.int32)
    by_col = jnp.zeros((ROWS, ROWS), jnp.int32)
    for j in range(ROWS):
        r = owner[j]
        at = (j % 2) * 16 + j // 2
        by_row = jnp.where(row == at, r, by_row)
        by_col = jnp.where(col == at, r, by_col)
    to_slots = jnp.where(by_row == col, 1.0, 0.0).astype(BF16)
    to_requests = jnp.where(by_col == row, 1.0, 0.0).astype(BF16)
    start = _nn(to_slots, hidden[...]).astype(BF16)
    states[0] = start[:16]
    states[1] = start[16:]

    len0 = lengths[owner[2 * mem]]
    len1 = lengths[owner[2 * mem + 1]]
    upper = lax.broadcasted_iota(jnp.int32, (8, 128), 0) < 4
    angles = jnp.where(upper, len0, len1).astype(F32) * freqs[...]
    cosine = jnp.cos(angles)
    sine = jnp.sin(angles)
    lane = lax.broadcasted_iota(jnp.int32, (8, 128), 1)
    sine = jnp.where(lane < 64, -sine, sine)

    from15 = pl.ds(1, 15)
    from7 = pl.ds(1, 7)
    far_first = (OFFSETS[:5], OFFSETS[5:11], OFFSETS[11:])
    near_first = far_first[::-1]

    def index(o):
        return o[0] * 4 + o[1]

    def columns(j):
        return pl.ds(pl.multiple_of(j * 128, 128), 128)

    handovers = [
        remote(states.at[2 + h], xout.at[h], sendx.at[h], recvx.at[h], section=1 - sec)
        for h in range(2)
    ]
    lengths_here = (len0, len1)
    scale = 1.0 / math.sqrt(HD)

    def up_to_attention(layer, h):
        x = states[2 * layer + h].astype(F32)
        scaled = (x * attn_gain[...].astype(F32)).astype(BF16)
        squares = jnp.sum(x * x, axis=1, keepdims=True)
        if h == 0:
            for c in loads[:3]:
                c.wait()
            if layer == 0:
                for c in loads[3:]:
                    c.start()
        part = _nn(scaled, wqkv[...])
        wide = sw1.at[h]
        for k in range(10):
            wide[pl.ds(k, 16, stride=16), :] = part[:, k * 128 : (k + 1) * 128]
        high = squares.astype(BF16).astype(F32)
        wide[pl.ds(10, 16, stride=16), :] = jnp.broadcast_to(high, (16, 128))
        wide[pl.ds(11, 16, stride=16), :] = jnp.broadcast_to(squares - high, (16, 128))
        for k in range(12, 16):
            wide[pl.ds(k, 16, stride=16), :] = jnp.zeros((16, 128), F32)
        sb1[h] = wide[...].astype(BF16).reshape(16, 16, 128)
        if layer == 0 and h == 0:
            pl.semaphore_wait(barrier, 31)
        for o in OFFSETS:
            remote(
                sb1.at[h, peer(o)],
                rb1.at[h, slot_at(o)],
                send1.at[h],
                recv1.at[h],
                mem=peer(o),
            ).start()
        if layer == 0 and h == 1:
            for c in pushes[:3]:
                c.start()
        if layer == 1:
            handovers[h].start()
        yield

        heads = sb1[h, mem].astype(F32)
        wait_for(rb1.at[h, from15], recv1.at[h])
        for k in range(1, 16):
            heads = heads + rb1[h, k].astype(F32)
        heads = heads * lax.rsqrt((heads[10:11] + heads[11:12]) / D + EPS)
        c, n = cosine[4 * h : 4 * h + 1], sine[4 * h : 4 * h + 1]
        rotated = heads * c + pltpu.roll(heads, 64, 1) * n
        q = rotated[0:8].astype(BF16)
        new_key = rotated[8:9].astype(BF16).astype(F32)
        new_value = heads[9:10].astype(BF16).astype(F32)
        own_score = jnp.sum(q.astype(F32) * new_key, axis=1, keepdims=True) * scale
        loads[3 + 2 * h].wait()
        scores = _nt(q, kbuf[h]) * scale
        where = lax.broadcasted_iota(jnp.int32, (8, CTX), 1)
        scores = jnp.where(where < lengths_here[h], scores, -jnp.inf)
        peak = jnp.maximum(jnp.max(scores, axis=1, keepdims=True), own_score)
        soft = jnp.exp(scores - peak)
        own = jnp.exp(own_score - peak)
        total = jnp.sum(soft, axis=1, keepdims=True) + own
        loads[4 + 2 * h].wait()
        mixed = _nn(soft.astype(BF16), vbuf[h])
        mixed = mixed + own.astype(BF16).astype(F32) * new_value
        attended = (mixed / total).astype(BF16)
        sb2[h] = attended
        at = 2 * layer + h
        for o in OFFSETS:
            remote(
                sb2.at[h], rb2.at[at, mem], send2.at[h], recv2.at[at], section=1, mem=peer(o)
            ).start()
        if layer == 0:
            remote(
                sb2.at[h], rb2.at[at, mem], send2.at[h], recv2.at[at], section=1 - sec
            ).start()
            if h == 1:
                for c in pushes[3:]:
                    c.start()
        else:
            rb2[at, mem] = attended
        yield

    def rest_of(layer, h, drain=None):
        at = 2 * layer + h

        def ready(i):
            if h == 0 and layer == 0:
                pushes[i].wait_recv()
            elif h == 0:
                later[i].wait()

        def tp_send(part, sb, rb, sent, arrived):
            sb[at] = part.astype(BF16)
            for k in RING:
                remote(
                    sb.at[at], rb.at[at, tp], sent.at[at], arrived.at[at], tp=lax.rem(tp + k, 8)
                ).start()
            rb[at, tp] = sb[at]

        def tp_sum(rb, arrived):
            wait_for(rb.at[at, from7], arrived.at[at])
            total = rb[at, 0].astype(F32)
            for k in range(1, 8):
                total = total + rb[at, k].astype(F32)
            return total

        ready(0)
        if layer == 0:
            wait_for(rb2.at[at], recv2.at[at])
        else:
            wait_for(rb2.at[at, from15], recv2.at[at])
        fb2[h] = rb2[at].astype(F32).reshape(128, 128)
        wide = jnp.concatenate([fb2[h, pl.ds(k, 16, stride=8), :] for k in range(8)], axis=1)
        tp_send(_nn(wide.astype(BF16), wo[layer]), sb3, rb3, send3, recv3)
        yield

        x = states[at].astype(F32) + tp_sum(rb3, recv3)
        x = x.astype(BF16).astype(F32)

        ready(1)
        scaled = (x * ffn_gain[layer].astype(F32)).astype(BF16)
        squares = jnp.sum(x * x, axis=1, keepdims=True)
        packed = jnp.where(lane < 64, squares[0:8], squares[8:16])
        ssq[at] = packed
        ready(2)
        ready(3)

        def units(j):
            j = jnp.minimum(j, OWNERS - 1)
            both = jnp.concatenate([wg[layer, :, columns(j)], wu[layer, :, columns(j)]], axis=1)
            return _nn(scaled, both)

        for group in far_first:
            for o in group:
                sb4[at, index(o)] = units(peer(o)).astype(BF16)
            for o in group:

                @pl.when(peer(o) < OWNERS)
                def _(o=o):
                    remote(
                        sb4.at[at, index(o)],
                        rb4.at[at, slot_at(o)],
                        send4.at[at],
                        recv4.at[at, slot_at(o)],
                        mem=peer(o),
                    ).start()

            for o in group:
                remote(
                    ssq.at[at], rsq.at[at, slot_at(o)], sendq.at[at], recvq.at[at], mem=peer(o)
                ).start()
        sums = units(mem)
        yield

        @pl.when(mem < OWNERS)
        def _():
            own_units = sums
            for group in near_first:
                for k in [index(o) for o in group]:
                    wait_for(rb4.at[at, k], recv4.at[at, k])
                for k in [index(o) for o in group]:
                    own_units = own_units + rb4[at, k].astype(F32)
            wait_for(rsq.at[at, from15], recvq.at[at])
            mean = packed
            for k in range(1, 16):
                mean = mean + rsq[at, k]
            mean = lax.rsqrt(mean / D + EPS)
            factor = jnp.concatenate([mean[:, 0:1], mean[:, 64:65]], axis=0)
            own_units = own_units * factor
            gate, up = own_units[:, :128], own_units[:, 128:]
            here = (gate / (1.0 + jnp.exp(-gate)) * up).astype(BF16)
            sb5[at] = here
            rb5[at, mem] = here
            for o in OFFSETS:
                remote(
                    sb5.at[at],
                    rb5.at[at, mem],
                    send5.at[at],
                    recv5.at[at, slot_at(o)],
                    mem=peer(o),
                ).start()

        @pl.when(mem >= OWNERS)
        def _():
            wait_for(rsq.at[at, from15], recvq.at[at])
            rb5[at, mem] = jnp.zeros((16, 128), BF16)

        yield

        ready(4)
        part = jnp.zeros((16, 512), F32)
        for group in ([(0, 0)] + near_first[0],) + near_first[1:]:
            for o in group:
                if o != (0, 0):

                    @pl.when(peer(o) < OWNERS)
                    def _(o=o):
                        k = index(o)
                        wait_for(rb5.at[at, k], recv5.at[at, k])

                    @pl.when(peer(o) >= OWNERS)
                    def _(o=o):
                        rb5[at, peer(o)] = jnp.zeros((16, 128), BF16)

            theirs = jnp.concatenate([rb5[at, peer(o)] for o in group], axis=1)
            down = jnp.concatenate(
                [wd[layer, columns(jnp.minimum(peer(o), OWNERS - 1)), :] for o in group], axis=0
            )
            part = part + _nn(theirs, down)
        tp_send(part, sb6, rb6, send6, recv6)
        if drain is not None:
            drain()
        yield

        y = (x + tp_sum(rb6, recv6)).astype(BF16)
        if layer == 0:
            states[2 + h] = y
        else:
            xout[h] = y

    def side_by_side(chains):
        chains = list(chains)
        while chains:
            chains = [c for c in chains if next(c, True) is None]

    def drained():
        for h in range(2):
            wait_for(rb1.at[h, from15], send1.at[h])
            wait_for(rb2.at[h, from15], send2.at[h])
            handovers[h].wait_send()
        for at in range(4):
            wait_for(rb3.at[at, from7], send3.at[at])
            wait_for(rsq.at[at, from15], sendq.at[at])
            if at < 2:
                wait_for(rb6.at[at, from7], send6.at[at])

            @pl.when(mem < OWNERS)
            def _(at=at):
                wait_for(rb4.at[at, pl.ds(0, 13)], send4.at[at])
                wait_for(rb5.at[at, pl.ds(0, 15)], send5.at[at])

            @pl.when(mem >= OWNERS)
            def _(at=at):
                wait_for(rb4.at[at, pl.ds(0, 14)], send4.at[at])

    @pl.when(sec == 0)
    def _():
        side_by_side(up_to_attention(0, h) for h in range(2))
        for h in range(2):
            wait_for(rb1.at[h, from15], send1.at[h])
            wait_for(rb2.at[h], send2.at[h])
        for c in pushes:
            c.wait_send()
        for c in handovers:
            c.wait_recv()

    @pl.when(sec == 1)
    def _():
        for c in loads[3:] + later:
            c.start()
        pl.semaphore_wait(barrier, 23)

        def chain(h):
            yield from rest_of(0, h)
            yield from up_to_attention(1, h)
            yield from rest_of(1, h, drained if h == 1 else None)

        side_by_side(chain(h) for h in range(2))

    states_out = jnp.concatenate([xout[0], xout[1]], axis=0)
    out[0] = _nn(to_requests, states_out).astype(BF16)

    @pl.when(sec == 1)
    def _():
        for at in (2, 3):
            wait_for(rb6.at[at, from7], send6.at[at])


FREQS = (500000.0 ** (-(np.arange(64, dtype=np.float64) * 2.0) / 128)).astype(np.float32)
FREQS = np.concatenate([FREQS, FREQS])[None, :]


def per_device(hidden_in, lengths, owner_order, attn_gain, w_query, w_key, w_value, w_out,
               ffn_gain, w_gate, w_up, w_down, key_cache, value_cache):
    vmem = pl.BlockSpec(memory_space=pltpu.VMEM)
    hbm = pl.BlockSpec(memory_space=pl.ANY)
    V, S = pltpu.VMEM, pltpu.SemaphoreType.DMA
    return pl.pallas_call(
        kernel,
        out_shape=pltpu.VMEM((1, ROWS, 512), BF16),
        in_specs=[hbm] * 15,
        out_specs=vmem,
        scratch_shapes=[
            pltpu.SMEM((ROWS,), jnp.int32),
            pltpu.SMEM((ROWS,), jnp.int32),
            V((1, 128), F32),
            V((ROWS, 512), BF16),
            V((1, 512), BF16),
            V((2, 1, 512), BF16),
            V((512, 1280), BF16),
            V((2, CTX, 128), BF16),
            V((2, CTX, 128), BF16),
            V((2, 1024, 512), BF16),
            V((2, 512, 1792), BF16),
            V((2, 512, 1792), BF16),
            V((2, 1792, 512), BF16),
            V((4, 16, 512), BF16),
            V((2, 16, 512), BF16),
            V((2, 256, 128), F32),
            V((2, 16, 16, 128), BF16),
            V((2, 16, 16, 128), BF16),
            V((2, 8, 128), BF16),
            V((4, 16, 8, 128), BF16),
            V((2, 128, 128), F32),
            V((4, 16, 512), BF16),
            V((4, 8, 16, 512), BF16),
            V((4, 8, 128), F32),
            V((4, 16, 8, 128), F32),
            V((4, 16, 16, 256), BF16),
            V((4, 16, 16, 256), BF16),
            V((4, 16, 128), BF16),
            V((4, 16, 16, 128), BF16),
            V((4, 16, 512), BF16),
            V((4, 8, 16, 512), BF16),
            S((5,)),
            S((12,)),
            S((5,)),
            S((5,)),
            S((2,)),
            S((2,)),
            S((2,)),
            S((4,)),
            S((4,)),
            S((4,)),
            S((4,)),
            S((4,)),
            S((4,)),
            S((4, 16)),
            S((4,)),
            S((4, 16)),
            S((4,)),
            S((4,)),
            S((2,)),
            S((2,)),
        ],
        compiler_params=pltpu.CompilerParams(
            collective_id=0, has_side_effects=True, vmem_limit_bytes=56 << 20
        ),
    )(
        lengths, owner_order, jnp.asarray(FREQS), hidden_in, attn_gain, ffn_gain,
        w_query, w_key, w_value, w_out, w_gate, w_up, w_down, key_cache, value_cache,
    )


def solution(mesh):
    placed = (
        P(None, "mem"),
        P(),
        P(),
        P("section", "mem"),
        P("section", "mem", "tp"),
        P("section", "mem", "tp"),
        P("section", "mem", "tp"),
        P("section", "tp", "mem"),
        P("section", "mem"),
        P("section", "mem", "tp"),
        P("section", "mem", "tp"),
        P("section", "tp", "mem"),
        P("section", "mem", None, "tp"),
        P("section", "mem", None, "tp"),
    )
    return jax.shard_map(
        per_device, mesh=mesh, in_specs=placed, out_specs=P("section", None, "mem"), check_vma=False
    )
```

time: 72.3 us -> 66.5 us (0.920)
  Pallas kernels: 71.6 us -> 65.7 us
    pallas_call x1, Pallas kernels: 71.6 us -> 65.7 us  [per_device(): pl.pallas_call(kernel, out_shape=pltpu.VMEM((1, ROWS, 512), BF16), in_spe...]
where the time goes in v4:
time: 66.5 us; the launch traced here: 66.4 us
  Pallas kernels  65.7 us (99%)
    pallas_call x1, Pallas kernels, per_device(): pl.pallas_call(kernel, out_shape=pltpu.VMEM((1, ROWS, 512), BF16), in_spe...  65.7 us

profile of v4, /device:TPU:1, one launch (start us, length us, event | category | flops | bytes accessed | tf_op | source)
XLA Modules:
  0.0 66.4 jit_solution(8647789942113173652)
XLA Ops:
  0.0 65.7 %shard_map.145 = bf16[1,32,512]{2,1,0:T(8,128)(2,1)S(1)} custom-call(s32[32]{0:T(128)} %lengths_in.1, s32[32]{0:T(128)} %owner_in.1, f32[1,128]{1,0:T(1,128)} %constant.2.clone.freqs_in, bf16[32,512]{1,0:T(8,128)(2,1)} %hidden_in.1, bf16[1,512]{1,0:T(2,128)(2,1)} %attn_gain_in.1, bf16[1,512]{1,0:T(2,128)(2,1)} %ffn_gain_in.1, bf16[1,512,1024]{2,1,0:T(8,128)(2,1)} %w_query.1, ...), custom_call_target="tpu_custom_call" | custom-call | tf_op jit(solution)/shard_map/pallas_call | solution.py:516
  65.7 0.6 copy.17

commit v5 on v4

--- a/solution.py
+++ b/solution.py
@@ -180,6 +180,10 @@
         remote(s, d.at[0], push_send.at[i], push_recv.at[i], section=1 - sec)
         for i, (s, d) in enumerate(later)
     ]
+    moves = [
+        remote(s, d.at[2], push_send.at[5 + i], push_recv.at[5 + i], section=1 - sec)
+        for i, (s, d) in enumerate([(key_cache.at[0, 0], kbuf), (value_cache.at[0, 0], vbuf)])
+    ]
     later = [
         pltpu.make_async_copy(s, d.at[1], wsem.at[7 + i]) for i, (s, d) in enumerate(later)
     ]
@@ -213,6 +217,7 @@
     lane = lax.broadcasted_iota(jnp.int32, (8, 128), 1)
     sine = jnp.where(lane < 64, -sine, sine)
 
+    sw1[...] = jnp.zeros((2, 256, 128), F32)
     from15 = pl.ds(1, 15)
     from7 = pl.ds(1, 7)
     far_first = (OFFSETS[:5], OFFSETS[5:11], OFFSETS[11:])
@@ -231,7 +236,8 @@
     lengths_here = (len0, len1)
     scale = 1.0 / math.sqrt(HD)
 
-    def up_to_attention(layer, h):
+    def project(layer, h):
+        moved = layer == 0 and h == 0
         x = states[2 * layer + h].astype(F32)
         scaled = (x * attn_gain[...].astype(F32)).astype(BF16)
         squares = jnp.sum(x * x, axis=1, keepdims=True)
@@ -239,7 +245,7 @@
             for c in loads[:3]:
                 c.wait()
             if layer == 0:
-                for c in loads[3:]:
+                for c in loads[5:]:
                     c.start()
         part = _nn(scaled, wqkv[...])
         wide = sw1.at[h]
@@ -248,30 +254,44 @@
         high = squares.astype(BF16).astype(F32)
         wide[pl.ds(10, 16, stride=16), :] = jnp.broadcast_to(high, (16, 128))
         wide[pl.ds(11, 16, stride=16), :] = jnp.broadcast_to(squares - high, (16, 128))
-        for k in range(12, 16):
-            wide[pl.ds(k, 16, stride=16), :] = jnp.zeros((16, 128), F32)
         sb1[h] = wide[...].astype(BF16).reshape(16, 16, 128)
-        if layer == 0 and h == 0:
+        if layer == 0:
+            yield
+        if moved:
             pl.semaphore_wait(barrier, 31)
+        to = 2 if moved else h
+        where = {"section": 1} if moved else {}
         for o in OFFSETS:
             remote(
                 sb1.at[h, peer(o)],
-                rb1.at[h, slot_at(o)],
+                rb1.at[to, slot_at(o)],
                 send1.at[h],
-                recv1.at[h],
+                recv1.at[to],
                 mem=peer(o),
+                **where,
             ).start()
-        if layer == 0 and h == 1:
-            for c in pushes[:3]:
+        if moved:
+            remote(sb1.at[h, mem], rb1.at[2, 0], send1.at[h], recv1.at[2], section=1 - sec).start()
+            for c in moves:
+                c.start()
+        elif layer == 0:
+            for c in pushes[:2]:
                 c.start()
         if layer == 1:
             handovers[h].start()
         yield
 
-        heads = sb1[h, mem].astype(F32)
-        wait_for(rb1.at[h, from15], recv1.at[h])
+    def attend(layer, h):
+        moved = layer == 0 and h == 0
+        here = 2 if moved else h
+        if moved:
+            wait_for(rb1.at[2], recv1.at[2])
+            heads = rb1[2, 0].astype(F32)
+        else:
+            wait_for(rb1.at[h, from15], recv1.at[h])
+            heads = sb1[h, mem].astype(F32)
         for k in range(1, 16):
-            heads = heads + rb1[h, k].astype(F32)
+            heads = heads + rb1[here, k].astype(F32)
         heads = heads * lax.rsqrt((heads[10:11] + heads[11:12]) / D + EPS)
         c, n = cosine[4 * h : 4 * h + 1], sine[4 * h : 4 * h + 1]
         rotated = heads * c + pltpu.roll(heads, 64, 1) * n
@@ -279,31 +299,36 @@
         new_key = rotated[8:9].astype(BF16).astype(F32)
         new_value = heads[9:10].astype(BF16).astype(F32)
         own_score = jnp.sum(q.astype(F32) * new_key, axis=1, keepdims=True) * scale
-        loads[3 + 2 * h].wait()
-        scores = _nt(q, kbuf[h]) * scale
+        if moved:
+            moves[0].wait_recv()
+        else:
+            loads[3 + 2 * h].wait()
+        scores = _nt(q, kbuf[here]) * scale
         where = lax.broadcasted_iota(jnp.int32, (8, CTX), 1)
         scores = jnp.where(where < lengths_here[h], scores, -jnp.inf)
         peak = jnp.maximum(jnp.max(scores, axis=1, keepdims=True), own_score)
         soft = jnp.exp(scores - peak)
         own = jnp.exp(own_score - peak)
         total = jnp.sum(soft, axis=1, keepdims=True) + own
-        loads[4 + 2 * h].wait()
-        mixed = _nn(soft.astype(BF16), vbuf[h])
+        if moved:
+            moves[1].wait_recv()
+        else:
+            loads[4 + 2 * h].wait()
+        mixed = _nn(soft.astype(BF16), vbuf[here])
         mixed = mixed + own.astype(BF16).astype(F32) * new_value
         attended = (mixed / total).astype(BF16)
-        sb2[h] = attended
+        sb2[here] = attended
         at = 2 * layer + h
         for o in OFFSETS:
             remote(
-                sb2.at[h], rb2.at[at, mem], send2.at[h], recv2.at[at], section=1, mem=peer(o)
+                sb2.at[here], rb2.at[at, mem], send2.at[here], recv2.at[at], section=1, mem=peer(o)
             ).start()
-        if layer == 0:
+        if layer == 0 and not moved:
             remote(
                 sb2.at[h], rb2.at[at, mem], send2.at[h], recv2.at[at], section=1 - sec
             ).start()
-            if h == 1:
-                for c in pushes[3:]:
-                    c.start()
+            for c in pushes[2:]:
+                c.start()
         else:
             rb2[at, mem] = attended
         yield
@@ -333,7 +358,7 @@
             return total
 
         ready(0)
-        if layer == 0:
+        if layer == 0 and h == 1:
             wait_for(rb2.at[at], recv2.at[at])
         else:
             wait_for(rb2.at[at, from15], recv2.at[at])
@@ -454,8 +479,9 @@
     def drained():
         for h in range(2):
             wait_for(rb1.at[h, from15], send1.at[h])
-            wait_for(rb2.at[h, from15], send2.at[h])
             handovers[h].wait_send()
+        for k in range(3):
+            wait_for(rb2.at[k, from15], send2.at[k])
         for at in range(4):
             wait_for(rb3.at[at, from7], send3.at[at])
             wait_for(rsq.at[at, from15], sendq.at[at])
@@ -473,11 +499,15 @@
 
     @pl.when(sec == 0)
     def _():
-        side_by_side(up_to_attention(0, h) for h in range(2))
-        for h in range(2):
-            wait_for(rb1.at[h, from15], send1.at[h])
-            wait_for(rb2.at[h], send2.at[h])
-        for c in pushes:
+        def half1():
+            yield from project(0, 1)
+            yield from attend(0, 1)
+
+        side_by_side([project(0, 0), half1()])
+        wait_for(rb1.at[0], send1.at[0])
+        wait_for(rb1.at[0, from15], send1.at[1])
+        wait_for(rb2.at[0], send2.at[1])
+        for c in moves + pushes:
             c.wait_send()
         for c in handovers:
             c.wait_recv()
@@ -489,8 +519,13 @@
         pl.semaphore_wait(barrier, 23)
 
         def chain(h):
+            if h == 0:
+                yield from attend(0, 0)
+            else:
+                yield
             yield from rest_of(0, h)
-            yield from up_to_attention(1, h)
+            yield from project(1, h)
+            yield from attend(1, h)
             yield from rest_of(1, h, drained if h == 1 else None)
 
         side_by_side(chain(h) for h in range(2))
@@ -526,8 +561,8 @@
             V((1, 512), BF16),
             V((2, 1, 512), BF16),
             V((512, 1280), BF16),
-            V((2, CTX, 128), BF16),
-            V((2, CTX, 128), BF16),
+            V((3, CTX, 128), BF16),
+            V((3, CTX, 128), BF16),
             V((2, 1024, 512), BF16),
             V((2, 512, 1792), BF16),
             V((2, 512, 1792), BF16),
@@ -536,8 +571,8 @@
             V((2, 16, 512), BF16),
             V((2, 256, 128), F32),
             V((2, 16, 16, 128), BF16),
-            V((2, 16, 16, 128), BF16),
-            V((2, 8, 128), BF16),
+            V((3, 16, 16, 128), BF16),
+            V((3, 8, 128), BF16),
             V((4, 16, 8, 128), BF16),
             V((2, 128, 128), F32),
             V((4, 16, 512), BF16),
@@ -552,11 +587,11 @@
             V((4, 8, 16, 512), BF16),
             S((5,)),
             S((12,)),
-            S((5,)),
-            S((5,)),
+            S((7,)),
+            S((7,)),
             S((2,)),
-            S((2,)),
-            S((2,)),
+            S((3,)),
+            S((3,)),
             S((4,)),
             S((4,)),
             S((4,)),

time: 66.5 us -> 65.9 us (level)
  no operation moved by 1% of the time
where the time goes in v5:
time: 65.9 us; the launch traced here: 65.8 us
  Pallas kernels  65.1 us (99%)
    pallas_call x1, Pallas kernels, per_device(): pl.pallas_call(kernel, out_shape=pltpu.VMEM((1, ROWS, 512), BF16), in_spe...  65.1 us

profile of v5, /device:TPU:1, one launch (start us, length us, event | category | flops | bytes accessed | tf_op | source)
XLA Modules:
  0.0 65.8 jit_solution(7389889125962447676)
XLA Ops:
  0.0 65.1 %shard_map.145 = bf16[1,32,512]{2,1,0:T(8,128)(2,1)S(1)} custom-call(s32[32]{0:T(128)} %lengths_in.1, s32[32]{0:T(128)} %owner_in.1, f32[1,128]{1,0:T(1,128)} %constant.2.clone.freqs_in, bf16[32,512]{1,0:T(8,128)(2,1)} %hidden_in.1, bf16[1,512]{1,0:T(2,128)(2,1)} %attn_gain_in.1, bf16[1,512]{1,0:T(2,128)(2,1)} %ffn_gain_in.1, bf16[1,512,1024]{2,1,0:T(8,128)(2,1)} %w_query.1, ...), custom_call_target="tpu_custom_call" | custom-call | tf_op jit(solution)/shard_map/pallas_call | solution.py:551
  65.1 0.6 copy.17

commit v6 on v5

--- a/solution.py
+++ b/solution.py
@@ -115,6 +115,12 @@
     def peer(o):
         return lax.rem(my + o[0], 4) * 4 + lax.rem(mx + o[1], 4)
 
+    peers = {o: peer(o) for o in [(0, 0)] + OFFSETS}
+    ring = {k: lax.rem(tp + k, 8) for k in RING}
+
+    def peer(o):
+        return peers[o]
+
     def slot_at(o):
         return ((4 - o[0]) % 4) * 4 + (4 - o[1]) % 4
 
@@ -220,7 +226,7 @@
     sw1[...] = jnp.zeros((2, 256, 128), F32)
     from15 = pl.ds(1, 15)
     from7 = pl.ds(1, 7)
-    far_first = (OFFSETS[:5], OFFSETS[5:11], OFFSETS[11:])
+    far_first = (OFFSETS[:1], OFFSETS[1:5], OFFSETS[5:11], OFFSETS[11:])
     near_first = far_first[::-1]
 
     def index(o):
@@ -346,7 +352,7 @@
             sb[at] = part.astype(BF16)
             for k in RING:
                 remote(
-                    sb.at[at], rb.at[at, tp], sent.at[at], arrived.at[at], tp=lax.rem(tp + k, 8)
+                    sb.at[at], rb.at[at, tp], sent.at[at], arrived.at[at], tp=ring[k]
                 ).start()
             rb[at, tp] = sb[at]
 

time: 65.9 us -> 65.8 us (level)
  no operation moved by 1% of the time
where the time goes in v6:
time: 65.8 us; the launch traced here: 65.7 us
  Pallas kernels  65.1 us (99%)
    pallas_call x1, Pallas kernels, per_device(): pl.pallas_call(kernel, out_shape=pltpu.VMEM((1, ROWS, 512), BF16), in_spe...  65.1 us

profile of v6, /device:TPU:1, one launch (start us, length us, event | category | flops | bytes accessed | tf_op | source)
XLA Modules:
  0.0 65.7 jit_solution(11830178379302263173)
XLA Ops:
  0.0 65.1 %shard_map.145 = bf16[1,32,512]{2,1,0:T(8,128)(2,1)S(1)} custom-call(s32[32]{0:T(128)} %lengths_in.1, s32[32]{0:T(128)} %owner_in.1, f32[1,128]{1,0:T(1,128)} %constant.2.clone.freqs_in, bf16[32,512]{1,0:T(8,128)(2,1)} %hidden_in.1, bf16[1,512]{1,0:T(2,128)(2,1)} %attn_gain_in.1, bf16[1,512]{1,0:T(2,128)(2,1)} %ffn_gain_in.1, bf16[1,512,1024]{2,1,0:T(8,128)(2,1)} %w_query.1, ...), custom_call_target="tpu_custom_call" | custom-call | tf_op jit(solution)/shard_map/pallas_call | solution.py:557
  65.1 0.6 copy.17
